TPU v7x, 128 devices: a whole 4x4x4 slice. The times are simulated.
128 devices in a mesh: gx: 16 (over z, y), yz: 8 (over x, core).
Axes of the slice: x: 4, y: 4, z: 4, core: 2. Of those that a mesh axis runs over, the one named last changes fastest.
Arguments:
- cell_matrix: bfloat16 [32, 256, 256, 256], P('gx', 'yz'), as said below
- x_coupling: bfloat16 [32, 256, 128], P('gx', 'yz'), may hold values from 0.5 to 2
- y_coupling: bfloat16 [32, 256, 128], P('gx', 'yz'), may hold values from 0.5 to 2
- cell_interp: bfloat16 [32, 256, 256, 128], P('gx', 'yz'), may hold values from -0.375 to 0.375
- cell_skel: int32 [32, 256, 128], P('gx', 'yz'), may hold values from 0 to 255, as said below
- cell_rank: int32 [32, 256], P('gx', 'yz'), may hold values from 64 to 128, as said below
- x_face_interp: bfloat16 [32, 256, 256, 128], P('gx', 'yz'), may hold values from -0.375 to 0.375
- x_face_skel: int32 [32, 256, 128], P('gx', 'yz'), may hold values from 0 to 255, as said below
- x_face_rank: int32 [32, 256], P('gx', 'yz'), may hold values from 64 to 128, as said below
- y_face_interp: bfloat16 [32, 256, 256, 128], P('gx', 'yz'), may hold values from -0.375 to 0.375
- y_face_skel: int32 [32, 256, 128], P('gx', 'yz'), may hold values from 0 to 255, as said below
- y_face_rank: int32 [32, 256], P('gx', 'yz'), may hold values from 64 to 128, as said below
Outputs:
- x_face_block: bfloat16 [32, 256, 128, 128], P('gx', 'yz')
- y_face_block: bfloat16 [32, 256, 128, 128], P('gx', 'yz')
Inputs may be any that keep to these rules, and one draw needn't show every extreme that they name: `cell_skel`: each row names 128 distinct unknowns of a cell block. `cell_rank`: the slots of cell_skel below a cell's rank are its live skeleton. `x_face_skel`: each row names 128 distinct unknowns of the face's two cells. `x_face_rank`: the slots of x_face_skel below a face's rank are its live skeleton. `y_face_skel`: each row names 128 distinct unknowns of the face's two cells. `y_face_rank`: the slots of y_face_skel below a face's rank are its live skeleton. `cell_matrix`: symmetric.
All inputs are finite; a program needn't handle non-finite values.
Results may differ from a plain program's by a relative error of at most 0.0053.
Values may be sent and summed in bfloat16 or wider, within the bound.
A program may use at most 128 MiB of HBM per device.

v0:
```python
import jax
import jax.numpy as jnp
from jax import lax
from jax.sharding import PartitionSpec as P


def passed_along(x, axis, by):
    devices = lax.axis_size(axis)
    pairs = [(i, i + by) for i in range(devices) if 0 <= i + by < devices]
    return lax.ppermute(x, axis, pairs)


def make_basis(skel_list, rank_list, interp):
    row_count = interp.shape[-2]
    slot_count = skel_list.shape[-1]
    slot_index = lax.broadcasted_iota(jnp.int32, skel_list.shape, skel_list.ndim - 1)
    live_slots = slot_index < rank_list[..., None]
    row_index = lax.broadcasted_iota(
        jnp.int32, skel_list.shape[:-1] + (row_count, slot_count), skel_list.ndim - 1
    )
    picked_rows = (row_index == skel_list[..., None, :]) & live_slots[..., None, :]
    kept_rows = jnp.any(picked_rows, axis=-1, keepdims=True)
    interp_part = jnp.where(live_slots[..., None, :], interp.astype(jnp.float32), jnp.float32(0.0))
    return jnp.where(
        picked_rows, jnp.float32(1.0), jnp.where(kept_rows, jnp.float32(0.0), interp_part)
    ).astype(jnp.bfloat16)


def project(matrix, left_basis, right_basis):
    inner_prod = jnp.einsum(
        "...ij,...jk->...ik", matrix, right_basis, preferred_element_type=jnp.float32
    ).astype(jnp.bfloat16)
    return jnp.einsum(
        "...ji,...jk->...ik", left_basis, inner_prod, preferred_element_type=jnp.float32
    )


def coupling_link(conduct, own_basis, right_basis):
    half_rows = own_basis.shape[-2] // 2
    scaled = (
        -conduct.astype(jnp.float32)[..., None]
        * right_basis[..., :half_rows, :].astype(jnp.float32)
    ).astype(jnp.bfloat16)
    return jnp.einsum(
        "...ji,...jk->...ik",
        own_basis[..., half_rows:, :],
        scaled,
        preferred_element_type=jnp.float32,
    )


def face_matrix(left_block, link_block, right_block):
    upper_half = jnp.concatenate([left_block, link_block], axis=-1)
    lower_half = jnp.concatenate([jnp.swapaxes(link_block, -1, -2), right_block], axis=-1)
    return jnp.concatenate([upper_half, lower_half], axis=-2)


def body(
    cell_matrix,
    x_coupling,
    y_coupling,
    cell_interp,
    cell_skel,
    cell_rank,
    x_face_interp,
    x_face_skel,
    x_face_rank,
    y_face_interp,
    y_face_skel,
    y_face_rank,
):
    cell_basis = make_basis(cell_skel, cell_rank, cell_interp)
    schur_block = project(cell_matrix, cell_basis, cell_basis).astype(jnp.bfloat16)
    x_basis = make_basis(x_face_skel, x_face_rank, x_face_interp)
    y_basis = make_basis(y_face_skel, y_face_rank, y_face_interp)
    y_basis_in, y_schur_in = passed_along((cell_basis[:, :1], schur_block[:, :1]), "yz", -1)
    right_y_basis = jnp.concatenate([cell_basis[:, 1:], y_basis_in], axis=1)
    right_y_schur = jnp.concatenate([schur_block[:, 1:], y_schur_in], axis=1)
    y_link = coupling_link(y_coupling, cell_basis, right_y_basis).astype(jnp.bfloat16)
    y_face_block = project(
        face_matrix(schur_block, y_link, right_y_schur), y_basis, y_basis
    ).astype(jnp.bfloat16)
    x_basis_in, x_schur_in = passed_along((cell_basis[:1], schur_block[:1]), "gx", -1)
    right_x_basis = jnp.concatenate([cell_basis[1:], x_basis_in], axis=0)
    x_link = coupling_link(x_coupling, cell_basis, right_x_basis).astype(jnp.bfloat16)
    right_x_schur = jnp.concatenate([schur_block[1:], x_schur_in], axis=0)
    x_face_block = project(
        face_matrix(schur_block, x_link, right_x_schur), x_basis, x_basis
    ).astype(jnp.bfloat16)
    return (x_face_block, y_face_block)


def solution(mesh):
    return jax.shard_map(
        body,
        mesh=mesh,
        in_specs=(
            P("gx", "yz", None, None),
            P("gx", "yz", None),
            P("gx", "yz", None),
            P("gx", "yz", None, None),
            P("gx", "yz", None),
            P("gx", "yz"),
            P("gx", "yz", None, None),
            P("gx", "yz", None),
            P("gx", "yz"),
            P("gx", "yz", None, None),
            P("gx", "yz", None),
            P("gx", "yz"),
        ),
        out_specs=(P("gx", "yz", None, None), P("gx", "yz", None, None)),
        check_vma=False,
    )
```

profile of v0, /device:TPU:90, one launch (start us, length us, event | category | flops | bytes accessed | tf_op | source)
XLA Modules:
  0.0 124.1 jit_solution(7578423901301805351)
XLA Ops:
  1.4 6.4 %copy.15 = bf16[2,32,256,128]{2,3,1,0:T(8,128)(2,1)} copy(bf16[2,32,256,128]{3,2,1,0:T(8,128)(2,1)} %param.15) | data formatting | bytes 8388608 | tf_op args[3]
  7.8 2.8 %fusion.21 = pred[2,32,256]{2,1,0:T(8,128)(4,1)S(1)} fusion(s32[2,32,128]{2,1,0:T(8,128)S(1)} %copy-done.8, pred[2,32,128]{2,1,0:T(8,128)(4,1)S(1)} %iota_compare_fusion.4), kind=kLoop, calls=%fused_computation.27 | loop fusion | flops 6275072 | bytes 57344 | tf_op jit(solution)/shard_map/reduce_or | solution.py:22
  10.6 6.4 %select_convert_fusion.1 = bf16[2,32,256,128]{2,3,1,0:T(8,128)(2,1)S(1)} fusion(bf16[2,32,256,128]{2,3,1,0:T(8,128)(2,1)} %copy.15, s32[2,32,128]{2,1,0:T(8,128)S(1)} %copy-done.8, pred[2,32,256]{2,1,0:T(8,128)(4,1)S(1)} %fusion.21, pred[2,32,128]{2,1,0:T(8,128)(4,1)S(1)} %iota_compare_fusion.4), kind=kLoop, calls=%fused_computation.20 | loop fusion | flops 14680064 | bytes 8445952 | tf_op jit(solution)/shard_map/convert_element_type | solution.py:26
  17.0 2.0 %copy-done = bf16[2,32,256,128]{2,3,1,0:T(8,128)(2,1)} copy-done((bf16[2,32,256,128]{2,3,1,0:T(8,128)(2,1)}, bf16[2,32,256,128]{2,3,1,0:T(8,128)(2,1)S(1)}, u32[]{:S(2)}) %copy-start) | copy-done | bytes 4194328
  19.0 1.9 %collective-permute-start.2 = (bf16[2,1,256,128]{2,3,1,0:T(8,128)(2,1)S(1)}, bf16[2,1,256,128]{2,3,1,0:T(8,128)(2,1)S(1)}, u32[]{:S(2)}, u32[]{:S(2)}) collective-permute-start(bf16[2,1,256,128]{2,3,1,0:T(8,128)(2,1)S(1)} %slice.51), channel_id=1, source_target_pairs={{1,0},{2,1},{3,2},{4,3},{5,4},{6,5},{7,6},{9,8},{10,9},{11,10},{12... | collective-permute-start | bytes 393224 | tf_op jit(solution)/shard_map/ppermute | solution.py:10
  20.9 7.9 %fusion.58 = bf16[2,32,128,128]{2,3,1,0:T(8,128)(2,1)S(1)} fusion(bf16[2,32,256,128]{2,3,1,0:T(8,128)(2,1)} %copy-done, bf16[2,32,256,256]{3,2,1,0:T(8,128)(2,1)} %param.12), kind=kOutput, calls=%fused_computation.51 | convolution fusion | flops 1613758464 | bytes 14680064 | tf_op jit(solution)/shard_map/...ji,...jk->...ik/dot_general | solution.py:33
  28.9 2.6 %collective-permute-start.3 = (bf16[2,1,128,128]{2,3,1,0:T(8,128)(2,1)S(1)}, bf16[2,1,128,128]{2,3,1,0:T(8,128)(2,1)}, u32[]{:S(2)}, u32[]{:S(2)}) collective-permute-start(bf16[2,1,128,128]{2,3,1,0:T(8,128)(2,1)S(1)} %slice.53), channel_id=1, source_target_pairs={{1,0},{2,1},{3,2},{4,3},{5,4},{6,5},{7,6},{9,8},{10,9},{11,10},{12... | collective-permute-start | bytes 196616 | tf_op jit(solution)/shard_map/ppermute | solution.py:10
  31.4 4.8 %fusion.77 = (bf16[1,32,256,128]{2,3,1,0:T(8,128)(2,1)}, bf16[1,32,256,128]{2,3,1,0:T(8,128)(2,1)}) fusion(bf16[2,32,256,128]{2,3,1,0:T(8,128)(2,1)} %copy-done), kind=kLoop, calls=%fused_computation.67 | loop fusion | bytes 8388608 | tf_op jit(solution)/shard_map/slice | solution.py:84
  36.2 2.9 %collective-permute-start = (bf16[1,32,256,128]{2,3,1,0:T(8,128)(2,1)}, bf16[1,32,256,128]{2,3,1,0:T(8,128)(2,1)}, u32[]{:S(2)}, u32[]{:S(2)}) collective-permute-start(bf16[1,32,256,128]{2,3,1,0:T(8,128)(2,1)} %get-tuple-element.3), channel_id=1, source_target_pairs={{8,0},{16,8},{24,16},{32,24},{40,32},{48,40},{56,48},{64,56},{72,6... | collective-permute-start | bytes 6291464 | tf_op jit(solution)/shard_map/ppermute | solution.py:10
  40.3 2.7 %collective-permute-start.1 = (bf16[1,32,128,128]{2,3,1,0:T(8,128)(2,1)}, bf16[1,32,128,128]{2,3,1,0:T(8,128)(2,1)}, u32[]{:S(2)}, u32[]{:S(2)}) collective-permute-start(bf16[1,32,128,128]{2,3,1,0:T(8,128)(2,1)} %get-tuple-element.5), channel_id=1, source_target_pairs={{8,0},{16,8},{24,16},{32,24},{40,32},{48,40},{56,48},{64,56},{72,6... | collective-permute-start | bytes 3145736 | tf_op jit(solution)/shard_map/ppermute | solution.py:10
  43.0 2.2 %slice.50 = bf16[2,31,256,128]{2,3,1,0:T(8,128)(2,1)} slice(bf16[2,32,256,128]{2,3,1,0:T(8,128)(2,1)S(1)} %copy-done.1), slice={[0:2], [1:32], [0:256], [0:128]} | slice | bytes 8126464 | tf_op jit(solution)/shard_map/slice | solution.py:77
  45.3 6.4 %copy.20 = bf16[2,32,256,128]{2,3,1,0:T(8,128)(2,1)} copy(bf16[2,32,256,128]{3,2,1,0:T(8,128)(2,1)} %param.21) | data formatting | bytes 8388608 | tf_op args[9]
  51.7 6.4 %copy.14 = bf16[2,32,256,128]{2,3,1,0:T(8,128)(2,1)} copy(bf16[2,32,256,128]{3,2,1,0:T(8,128)(2,1)} %param.18) | data formatting | bytes 8388608 | tf_op args[6]
  58.1 3.4 %fusion.23 = pred[2,32,256]{2,1,0:T(8,128)(4,1)} fusion(s32[2,32,128]{2,1,0:T(8,128)S(1)} %copy-done.9, pred[2,32,128]{2,1,0:T(8,128)(4,1)S(1)} %iota_compare_fusion.3), kind=kLoop, calls=%fused_computation.29 | loop fusion | flops 6275072 | bytes 57344 | tf_op jit(solution)/shard_map/reduce_or | solution.py:22
  61.5 3.4 %fusion.19 = pred[2,32,256]{2,1,0:T(8,128)(4,1)} fusion(s32[2,32,128]{2,1,0:T(8,128)S(1)} %copy-done.10, pred[2,32,128]{2,1,0:T(8,128)(4,1)S(1)} %iota_compare_fusion.5), kind=kLoop, calls=%fused_computation.25 | loop fusion | flops 6275072 | bytes 57344 | tf_op jit(solution)/shard_map/reduce_or | solution.py:22
  64.9 5.1 %fusion.56 = bf16[2,32,128,128]{2,3,1,0:T(8,128)(2,1)} fusion(bf16[2,1,256,128]{2,3,1,0:T(8,128)(2,1)S(1)} %collective-permute-done.2, bf16[2,31,256,128]{2,3,1,0:T(8,128)(2,1)} %slice.50, f32[2,32,128]{2,1,0:T(8,128)S(1)} %convert_negate_fusion, bf16[2,32,256,128]{2,3,1,0:T(8,128)(2,1)} %copy-done), kind=kOutput, calls=%fused_computation.49 | convolution fusion | flops 275775488 | bytes 8421376 | tf_op jit(solution)/shard_map/...ji,...jk->...ik/dot_general | solution.py:44
  70.0 4.3 %copy.23 = bf16[2,32,128,128]{2,3,1,0:T(8,128)(2,1)} copy(bf16[2,32,128,128]{3,2,1,0:T(8,128)(2,1)} %bitcast.8) | data formatting | bytes 4194304 | tf_op jit(solution)/shard_map/convert_element_type | solution.py:79
  74.3 8.7 %fusion.98 = bf16[2,32,256,128]{3,2,1,0:T(8,128)(2,1)S(1)} fusion(bf16[2,32,128,128]{2,3,1,0:T(8,128)(2,1)} %copy-done.3, bf16[2,1,128,128]{2,3,1,0:T(8,128)(2,1)} %collective-permute-done.3, bf16[2,31,128,128]{2,3,1,0:T(8,128)(2,1)S(1)} %slice-done, bf16[2,32,128,128]{2,3,1,0:T(8,128)(2,1)} %copy.23, ...), kind=kOutput, calls=%fused_computation.31.clone.clone.clone.2 | convolution fusion | flops 1132462080 | bytes 16834560 | tf_op jit(solution)/shard_map/...ij,...jk->...ik/dot_general | solution.py:30
  83.1 5.5 %fusion.51 = bf16[2,32,128,128]{3,2,1,0:T(8,128)(2,1)} fusion(bf16[2,32,256,128]{2,3,1,0:T(8,128)(2,1)S(1)} %copy-done.7, s32[2,32,128]{2,1,0:T(8,128)S(1)} %copy-done.9, pred[2,32,256]{2,1,0:T(8,128)(4,1)S(1)} %copy-done.14, pred[2,32,128]{2,1,0:T(8,128)(4,1)S(1)} %iota_compare_fusion.3, bf16[2,32,256,128]{3,2,1,0:T(8,128)(2,1)S(1)} %fusion.98), kind=kOutput, calls=%fused_computation.48 | convolution fusion | flops 552599552 | bytes 10543104 | tf_op jit(solution)/shard_map/...ji,...jk->...ik/dot_general | solution.py:33
  89.3 4.2 %fusion.57 = bf16[2,32,128,128]{2,3,1,0:T(8,128)(2,1)} fusion(bf16[1,32,256,128]{2,3,1,0:T(8,128)(2,1)} %collective-permute-done, bf16[1,32,256,128]{2,3,1,0:T(8,128)(2,1)S(1)} %copy-done.5, f32[2,32,128]{2,1,0:T(8,128)S(1)} %convert_negate_fusion.1, bf16[2,32,256,128]{2,3,1,0:T(8,128)(2,1)S(1)} %copy-done.2), kind=kOutput, calls=%fused_computation.50 | convolution fusion | flops 275775488 | bytes 8421376 | tf_op jit(solution)/shard_map/...ji,...jk->...ik/dot_general | solution.py:44
  93.4 4.3 %copy.19 = bf16[2,32,128,128]{2,3,1,0:T(8,128)(2,1)} copy(bf16[2,32,128,128]{3,2,1,0:T(8,128)(2,1)} %bitcast.7) | data formatting | bytes 4194304 | tf_op jit(solution)/shard_map/convert_element_type | solution.py:85
  97.7 12.9 %collective-permute-done.1 = bf16[1,32,128,128]{2,3,1,0:T(8,128)(2,1)} collective-permute-done((bf16[1,32,128,128]{2,3,1,0:T(8,128)(2,1)}, bf16[1,32,128,128]{2,3,1,0:T(8,128)(2,1)}, u32[]{:S(2)}, u32[]{:S(2)}) %collective-permute-start.1) | collective-permute-done | bytes 1048608 | tf_op jit(solution)/shard_map/ppermute | solution.py:10
  110.7 8.0 %fusion.95 = bf16[2,32,256,128]{3,2,1,0:T(8,128)(2,1)S(1)} fusion(bf16[2,32,128,128]{2,3,1,0:T(8,128)(2,1)S(1)} %copy-done.4, bf16[1,32,128,128]{2,3,1,0:T(8,128)(2,1)} %collective-permute-done.1, bf16[1,32,128,128]{2,3,1,0:T(8,128)(2,1)S(1)} %get-tuple-element.4, bf16[2,32,128,128]{2,3,1,0:T(8,128)(2,1)} %copy.19, ...), kind=kOutput, calls=%fused_computation.34.clone.clone.clone.2 | convolution fusion | flops 1132462080 | bytes 16834560 | tf_op jit(solution)/shard_map/...ij,...jk->...ik/dot_general | solution.py:30
  118.6 5.5 %fusion.46 = bf16[2,32,128,128]{3,2,1,0:T(8,128)(2,1)} fusion(bf16[2,32,256,128]{2,3,1,0:T(8,128)(2,1)S(1)} %copy-done.6, s32[2,32,128]{2,1,0:T(8,128)S(1)} %copy-done.10, pred[2,32,256]{2,1,0:T(8,128)(4,1)S(1)} %copy-done.13, pred[2,32,128]{2,1,0:T(8,128)(4,1)S(1)} %iota_compare_fusion.5, bf16[2,32,256,128]{3,2,1,0:T(8,128)(2,1)S(1)} %fusion.95), kind=kOutput, calls=%fused_computation.47 | convolution fusion | flops 552599552 | bytes 10543104 | tf_op jit(solution)/shard_map/...ji,...jk->...ik/dot_general | solution.py:33
  (46 shorter events, 2.9 us)
Async XLA Ops:
  1.4 6.4 %copy-start.8 = (s32[2,32,128]{2,1,0:T(8,128)S(1)}, s32[2,32,128]{2,1,0:T(8,128)}, u32[]{:S(2)}) copy-start(s32[2,32,128]{2,1,0:T(8,128)} %param.16) | copy-start | bytes 98308
  17.0 2.0 %copy-start = (bf16[2,32,256,128]{2,3,1,0:T(8,128)(2,1)}, bf16[2,32,256,128]{2,3,1,0:T(8,128)(2,1)S(1)}, u32[]{:S(2)}) copy-start(bf16[2,32,256,128]{2,3,1,0:T(8,128)(2,1)S(1)} %select_convert_fusion.1) | copy-start | bytes 12582916
  19.0 45.9 %collective-permute-start.2 = (bf16[2,1,256,128]{2,3,1,0:T(8,128)(2,1)S(1)}, bf16[2,1,256,128]{2,3,1,0:T(8,128)(2,1)S(1)}, u32[]{:S(2)}, u32[]{:S(2)}) collective-permute-start(bf16[2,1,256,128]{2,3,1,0:T(8,128)(2,1)S(1)} %slice.51), channel_id=1, source_target_pairs={{1,0},{2,1},{3,2},{4,3},{5,4},{6,5},{7,6},{9,8},{10,9},{11,10},{12... | collective-permute-start | bytes 393224 | tf_op jit(solution)/shard_map/ppermute | solution.py:10
  28.8 16.3 %copy-start.3 = (bf16[2,32,128,128]{2,3,1,0:T(8,128)(2,1)}, bf16[2,32,128,128]{2,3,1,0:T(8,128)(2,1)S(1)}, u32[]{:S(2)}) copy-start(bf16[2,32,128,128]{2,3,1,0:T(8,128)(2,1)S(1)} %fusion.58) | copy-start | bytes 6291460
  28.9 45.4 %collective-permute-start.3 = (bf16[2,1,128,128]{2,3,1,0:T(8,128)(2,1)S(1)}, bf16[2,1,128,128]{2,3,1,0:T(8,128)(2,1)}, u32[]{:S(2)}, u32[]{:S(2)}) collective-permute-start(bf16[2,1,128,128]{2,3,1,0:T(8,128)(2,1)S(1)} %slice.53), channel_id=1, source_target_pairs={{1,0},{2,1},{3,2},{4,3},{5,4},{6,5},{7,6},{9,8},{10,9},{11,10},{12... | collective-permute-start | bytes 196616 | tf_op jit(solution)/shard_map/ppermute | solution.py:10
  36.2 6.8 %copy-start.1 = (bf16[2,32,256,128]{2,3,1,0:T(8,128)(2,1)S(1)}, bf16[2,32,256,128]{2,3,1,0:T(8,128)(2,1)}, u32[]{:S(2)}) copy-start(bf16[2,32,256,128]{2,3,1,0:T(8,128)(2,1)} %copy-done) | copy-start | bytes 12582916
  36.2 53.1 %collective-permute-start = (bf16[1,32,256,128]{2,3,1,0:T(8,128)(2,1)}, bf16[1,32,256,128]{2,3,1,0:T(8,128)(2,1)}, u32[]{:S(2)}, u32[]{:S(2)}) collective-permute-start(bf16[1,32,256,128]{2,3,1,0:T(8,128)(2,1)} %get-tuple-element.3), channel_id=1, source_target_pairs={{8,0},{16,8},{24,16},{32,24},{40,32},{48,40},{56,48},{64,56},{72,6... | collective-permute-start | bytes 6291464 | tf_op jit(solution)/shard_map/ppermute | solution.py:10
  40.3 4.8 %copy-start.11 = (bf16[2,32,128]{2,1,0:T(8,128)(2,1)S(1)}, bf16[2,32,128]{2,1,0:T(8,128)(2,1)}, u32[]{:S(2)}) copy-start(bf16[2,32,128]{2,1,0:T(8,128)(2,1)} %param.14) | copy-start | bytes 49156
  40.3 4.9 %copy-start.15 = (s32[2,32]{1,0:T(2,128)S(1)}, s32[2,32]{1,0:T(2,128)}, u32[]{:S(2)}) copy-start(s32[2,32]{1,0:T(2,128)} %param.23) | copy-start | bytes 772
  40.3 70.3 %collective-permute-start.1 = (bf16[1,32,128,128]{2,3,1,0:T(8,128)(2,1)}, bf16[1,32,128,128]{2,3,1,0:T(8,128)(2,1)}, u32[]{:S(2)}, u32[]{:S(2)}) collective-permute-start(bf16[1,32,128,128]{2,3,1,0:T(8,128)(2,1)} %get-tuple-element.5), channel_id=1, source_target_pairs={{8,0},{16,8},{24,16},{32,24},{40,32},{48,40},{56,48},{64,56},{72,6... | collective-permute-start | bytes 3145736 | tf_op jit(solution)/shard_map/ppermute | solution.py:10
  45.3 6.4 %copy-start.16 = (s32[2,32]{1,0:T(2,128)S(1)}, s32[2,32]{1,0:T(2,128)}, u32[]{:S(2)}) copy-start(s32[2,32]{1,0:T(2,128)} %param.20) | copy-start | bytes 772
  51.7 6.4 %copy-start.9 = (s32[2,32,128]{2,1,0:T(8,128)S(1)}, s32[2,32,128]{2,1,0:T(8,128)}, u32[]{:S(2)}) copy-start(s32[2,32,128]{2,1,0:T(8,128)} %param.22) | copy-start | bytes 98308
  51.7 9.8 %copy-start.10 = (s32[2,32,128]{2,1,0:T(8,128)S(1)}, s32[2,32,128]{2,1,0:T(8,128)}, u32[]{:S(2)}) copy-start(s32[2,32,128]{2,1,0:T(8,128)} %param.19) | copy-start | bytes 98308
  51.7 13.2 %copy-start.12 = (bf16[2,32,128]{2,1,0:T(8,128)(2,1)S(1)}, bf16[2,32,128]{2,1,0:T(8,128)(2,1)}, u32[]{:S(2)}) copy-start(bf16[2,32,128]{2,1,0:T(8,128)(2,1)} %param.13) | copy-start | bytes 49156
  70.0 4.3 %slice-start = ((bf16[2,32,128,128]{2,3,1,0:T(8,128)(2,1)}), bf16[2,31,128,128]{2,3,1,0:T(8,128)(2,1)S(1)}, s32[]{:S(2)}) async-start(bf16[2,32,128,128]{2,3,1,0:T(8,128)(2,1)} %copy-done.3), calls=%async_computation | async-start | bytes 4063232 | tf_op jit(solution)/shard_map/slice | solution.py:78
  70.0 4.3 %copy-start.14 = (pred[2,32,256]{2,1,0:T(8,128)(4,1)S(1)}, pred[2,32,256]{2,1,0:T(8,128)(4,1)}, u32[]{:S(2)}) copy-start(pred[2,32,256]{2,1,0:T(8,128)(4,1)} %fusion.23) | copy-start | bytes 49156
  74.3 8.8 %copy-start.7 = (bf16[2,32,256,128]{2,3,1,0:T(8,128)(2,1)S(1)}, bf16[2,32,256,128]{2,3,1,0:T(8,128)(2,1)}, u32[]{:S(2)}) copy-start(bf16[2,32,256,128]{2,3,1,0:T(8,128)(2,1)} %copy.20) | copy-start | bytes 12582916
  83.1 6.2 %copy-start.2 = (bf16[2,32,256,128]{2,3,1,0:T(8,128)(2,1)S(1)}, bf16[2,32,256,128]{2,3,1,0:T(8,128)(2,1)}, u32[]{:S(2)}) copy-start(bf16[2,32,256,128]{2,3,1,0:T(8,128)(2,1)} %copy-done) | copy-start | bytes 12582916
  83.1 6.2 %copy-start.5 = (bf16[1,32,256,128]{2,3,1,0:T(8,128)(2,1)S(1)}, bf16[1,32,256,128]{2,3,1,0:T(8,128)(2,1)}, u32[]{:S(2)}) copy-start(bf16[1,32,256,128]{2,3,1,0:T(8,128)(2,1)} %get-tuple-element.2) | copy-start | bytes 6291460
  93.4 17.2 %copy-start.4 = (bf16[2,32,128,128]{2,3,1,0:T(8,128)(2,1)S(1)}, bf16[2,32,128,128]{2,3,1,0:T(8,128)(2,1)}, u32[]{:S(2)}) copy-start(bf16[2,32,128,128]{2,3,1,0:T(8,128)(2,1)} %copy-done.3) | copy-start | bytes 6291460
  93.4 17.2 %copy-start.13 = (pred[2,32,256]{2,1,0:T(8,128)(4,1)S(1)}, pred[2,32,256]{2,1,0:T(8,128)(4,1)}, u32[]{:S(2)}) copy-start(pred[2,32,256]{2,1,0:T(8,128)(4,1)} %fusion.19) | copy-start | bytes 49156
  110.7 8.0 %copy-start.6 = (bf16[2,32,256,128]{2,3,1,0:T(8,128)(2,1)S(1)}, bf16[2,32,256,128]{2,3,1,0:T(8,128)(2,1)}, u32[]{:S(2)}) copy-start(bf16[2,32,256,128]{2,3,1,0:T(8,128)(2,1)} %copy.14) | copy-start | bytes 12582916
where the time goes:
time: 126 us; the launch traced here: 124 us
  matrix products  44.8 us (36%)
  local copies, waits for them, and re-layouts  37.8 us (30%)
  other arithmetic  17 us (13%)
  waiting for transfers between devices  13.6 us (11%)
  starting transfers between devices  10 us (8%)
    unnamed x37, local copies, waits for them, and re-layouts  21.1 us
    dot_general x3, matrix products, project(): jnp.einsum('...ji,...jk->...ik', left_basis, inner_prod, preferred_elemen...  18.9 us
    dot_general x2, matrix products, project(): jnp.einsum('...ij,...jk->...ik', matrix, right_basis, preferred_element_t...  16.7 us
    ppermute x4, waiting for transfers between devices, passed_along(): return lax.ppermute(x, axis, pairs)  13.6 us
    ppermute x4, starting transfers between devices, passed_along(): return lax.ppermute(x, axis, pairs)  10 us
    reduce_or x3, other arithmetic, make_basis(): kept_rows = jnp.any(picked_rows, axis=-1, keepdims=True)  9.64 us
    dot_general x2, matrix products, coupling_link(): jnp.einsum('...ji,...jk->...ik', own_basis[..., half_rows:, :], scaled, p...  9.24 us
    convert_element_type x1, other arithmetic, make_basis(): return jnp.where(picked_rows, jnp.float32(1.0), jnp.where(kept_rows, jnp....  6.4 us
  transfers between devices with their start and end apart: 4, of which 2 were waited for; matrix products, arithmetic and copies ran while one was open for 55% of the time, Pallas kernels for 0%

commit v1 on v0

v1 whole, which is shorter than its diff:
```python
import functools

import jax
import jax.numpy as jnp
from jax import lax
from jax.experimental import pallas as pl
from jax.experimental.pallas import tpu as pltpu
from jax.sharding import PartitionSpec as P

F32, BF16 = jnp.float32, jnp.bfloat16
ROWS = (((1,), (1,)), ((), ()))
CB = 8
CM = 4


def passed_along(x, axis, by):
    devices = lax.axis_size(axis)
    pairs = [(i, i + by) for i in range(devices) if 0 <= i + by < devices]
    return lax.ppermute(x, axis, pairs)


def dot(a, b):
    return jnp.dot(a, b, preferred_element_type=F32)


def dot_t(a, b):
    return lax.dot_general(a, b, ROWS, preferred_element_type=F32)


def basis_t(column, interp):
    across = interp.T.astype(F32)
    lanes = lax.broadcasted_iota(jnp.int32, across.shape, 1).astype(F32)
    picked = lanes == column
    kept = jnp.max(jnp.where(picked, 1.0, 0.0), axis=0, keepdims=True)
    rest = jnp.where((kept > 0.0) | (column < 0.0), 0.0, across)
    return jnp.where(picked, 1.0, rest).astype(BF16)


def schur_t(basis, matrix):
    inner = dot(basis, matrix).astype(BF16)
    return dot_t(inner, basis).astype(BF16)


def link_of(own_bottom, conduct, right_top):
    scaled = (right_top.astype(F32) * -conduct).astype(BF16)
    return dot_t(own_bottom, scaled).astype(BF16)


def face_of(basis, left_t, link, right_t):
    upper = jnp.concatenate([left_t, link], axis=1)
    lower = jnp.concatenate([link.T, right_t], axis=1)
    inner = dot(basis, jnp.concatenate([upper, lower], axis=0)).astype(BF16)
    return dot_t(basis, inner).astype(BF16)


def columns_of(lists):
    return lists.T


def row_basis_kernel(list_ref, interp_ref, basis_ref, top_ref):
    columns = columns_of(list_ref[...])
    for c in range(CB):
        basis = basis_t(columns[:, c : c + 1], interp_ref[c])
        basis_ref[c] = basis
        top_ref[c] = basis[:, :128]


def packed_into(out_ref, at, first, second):
    down = lax.broadcasted_iota(jnp.int32, (128, 128), 0)
    across = lax.broadcasted_iota(jnp.int32, (128, 128), 1)
    out_ref[at * 128 : at * 128 + 128] = jnp.where(down <= across, first, second)
    diagonal = jnp.where(down == across, second.astype(F32), 0.0)
    return jnp.sum(diagonal, axis=0, keepdims=True)


def row_schur_kernel(
    basis_ref, matrix_ref, list_ref, interp_ref, corner_ref, schur_ref, early_ref, late_ref, edge_ref
):
    step = pl.program_id(0)
    blocks = [schur_t(basis_ref[c], matrix_ref[c]) for c in range(CB)]
    for c in range(CB):
        schur_ref[c] = blocks[c]

    def pack(out_ref):
        rows = [packed_into(out_ref, at, blocks[2 * at], blocks[2 * at + 1]) for at in range(CB // 2)]
        rows.append(jnp.zeros((16 - CB // 2, 128), F32))
        out_ref[CB // 2 * 128 :] = jnp.concatenate(rows, axis=0).astype(BF16)

    @pl.when(step < 3)
    def _():
        pack(early_ref)

    @pl.when(step == 3)
    def _():
        pack(late_ref)

    @pl.when(step == 0)
    def _():
        edge_ref[0, :128] = basis_ref[0, :, :128]
        edge_ref[0, 128:] = blocks[0]
        basis = basis_t(columns_of(list_ref[...])[:, :1], interp_ref[...])
        edge_ref[1, :128] = basis[:, :128]
        edge_ref[1, 128:] = schur_t(basis, corner_ref[...])


def main_kernel(
    list_ref,
    basis0_ref,
    schur0_ref,
    matrix_ref,
    interp_ref,
    x_interp_ref,
    y_interp_ref,
    x_conduct_ref,
    y_conduct_ref,
    x_face_ref,
    y_face_ref,
    bottom1_ref,
    schur1_ref,
    x_basis1_ref,
    next_top,
    next_schur,
):
    lists = columns_of(list_ref[...])

    def column(kind, row, c):
        at = (kind * 2 + row) * CM + c
        return lists[:, at : at + 1]

    tops = [[None] * CM, [None] * CM]
    bottoms = [[None] * CM, [None] * CM]
    schurs = [[None] * CM, [None] * CM]
    for c in range(CM):
        basis = basis_t(column(0, 1, c), interp_ref[c])
        block = schur_t(basis, matrix_ref[c])
        tops[1][c], bottoms[1][c], schurs[1][c] = basis[:, :128], basis[:, 128:], block
        bottom1_ref[c] = basis[:, 128:]
        schur1_ref[c] = block
        tops[0][c], bottoms[0][c] = basis0_ref[c, :, :128], basis0_ref[c, :, 128:]
        schurs[0][c] = schur0_ref[c]
        x_basis1_ref[c] = basis_t(column(1, 1, c), x_interp_ref[1, c])
    for c in range(CM):
        link = link_of(bottoms[0][c], x_conduct_ref[c : c + 1], tops[1][c])
        x_basis = basis_t(column(1, 0, c), x_interp_ref[0, c])
        x_face_ref[c] = face_of(x_basis, schurs[0][c], link, schurs[1][c])
        for row in range(2):
            last = c == CM - 1
            right_top = next_top[row] if last else tops[row][c + 1]
            right_schur = next_schur[row] if last else schurs[row][c + 1]
            at = row * CM + c
            link = link_of(bottoms[row][c], y_conduct_ref[at : at + 1], right_top)
            y_basis = basis_t(column(2, row, c), y_interp_ref[row, c])
            y_face_ref[row, c] = face_of(y_basis, schurs[row][c], link, right_schur)
    for row in range(2):
        next_top[row] = tops[row][0]
        next_schur[row] = schurs[row][0]


def edge_kernel(
    list_ref, bottom0_ref, bottom1_ref, schur0_ref, schur1_ref, edge_ref, interp_ref, conduct_ref, face_in, face_ref
):
    del face_in
    lists = columns_of(list_ref[...])
    for row, (bottom_ref, schur_ref) in enumerate(((bottom0_ref, schur0_ref), (bottom1_ref, schur1_ref))):
        link = link_of(bottom_ref[...], conduct_ref[row : row + 1], edge_ref[row, :128])
        basis = basis_t(lists[:, row : row + 1], interp_ref[row])
        face_ref[row] = face_of(basis, schur_ref[...], link, edge_ref[row, 128:])


def last_kernel(bottom_ref, schur_ref, basis_ref, conduct_ref, top_ref, packed_ref, face_in, face_ref):
    del face_in
    down = lax.broadcasted_iota(jnp.int32, (128, 128), 0)
    across = lax.broadcasted_iota(jnp.int32, (128, 128), 1)
    for at in range(CB // 2):
        packed = packed_ref[at * 128 : at * 128 + 128]
        turned = packed.T
        diagonal = packed_ref[CB // 2 * 128 : CB // 2 * 128 + 16][at : at + 1]
        first = jnp.where(down <= across, packed, turned)
        second = jnp.where(down > across, packed, turned)
        second = jnp.where(down == across, jnp.broadcast_to(diagonal, (128, 128)), second)
        for c, right in ((2 * at, first), (2 * at + 1, second)):
            link = link_of(bottom_ref[c], conduct_ref[c : c + 1], top_ref[c])
            face_ref[c] = face_of(basis_ref[c], schur_ref[c], link, right)


PARAMS = pltpu.CompilerParams(vmem_limit_bytes=48 << 20)


def cost(flops, size):
    return pl.CostEstimate(flops=flops, bytes_accessed=size, transcendentals=0)


def spec(*args):
    return pl.BlockSpec(*args)


def shape(*sizes):
    return jax.ShapeDtypeStruct(sizes, BF16)


def body(
    cell_matrix,
    x_coupling,
    y_coupling,
    cell_interp,
    cell_skel,
    cell_rank,
    x_face_interp,
    x_face_skel,
    x_face_rank,
    y_face_interp,
    y_face_skel,
    y_face_rank,
):
    def marked(skel, rank):
        slots = lax.broadcasted_iota(jnp.int32, skel.shape, 2)
        return jnp.where(slots < rank[..., None], skel, -1).astype(F32)

    NJ = cell_skel.shape[1]
    cell_list = marked(cell_skel, cell_rank)
    x_list = marked(x_face_skel, x_face_rank)
    y_list = marked(y_face_skel, y_face_rank)

    basis0, top0 = pl.pallas_call(
        row_basis_kernel,
        grid=(NJ // CB,),
        in_specs=[
            spec((None, CB, 128), lambda j: (0, j, 0)),
            spec((None, CB, 256, 128), lambda j: (0, j, 0, 0)),
        ],
        out_specs=[spec((CB, 128, 256), lambda j: (j, 0, 0)), spec((CB, 128, 128), lambda j: (j, 0, 0))],
        out_shape=[shape(NJ, 128, 256), shape(NJ, 128, 128)],
        compiler_params=PARAMS,
        cost_estimate=cost(1 << 24, 5 << 20),
        name="row_basis",
    )(cell_list, cell_interp)
    top_in = passed_along(top0, "gx", -1)

    packed = (CB // 2) * 128 + 16
    schur0, early, late, edge = pl.pallas_call(
        row_schur_kernel,
        grid=(NJ // CB,),
        in_specs=[
            spec((CB, 128, 256), lambda j: (j, 0, 0)),
            spec((None, CB, 256, 256), lambda j: (0, j, 0, 0)),
            spec((None, 8, 128), lambda j: (1, 0, 0)),
            spec((None, None, 256, 128), lambda j: (1, 0, 0, 0)),
            spec((None, None, 256, 256), lambda j: (1, 0, 0, 0)),
        ],
        out_specs=[
            spec((CB, 128, 128), lambda j: (j, 0, 0)),
            spec((None, packed, 128), lambda j: (jnp.minimum(j, 2), 0, 0)),
            spec((None, packed, 128), lambda j: (0, 0, 0)),
            spec((2, 256, 128), lambda j: (0, 0, 0)),
        ],
        out_shape=[shape(NJ, 128, 128), shape(3, packed, 128), shape(1, packed, 128), shape(2, 256, 128)],
        compiler_params=PARAMS,
        cost_estimate=cost(1 << 30, 8 << 20),
        name="row_schur",
    )(basis0, cell_matrix, cell_list, cell_interp, cell_matrix)
    early_in = passed_along(early, "gx", -1)
    edge_in = passed_along(edge, "yz", -1)
    late_in = passed_along(late, "gx", -1)

    steps = NJ // CM
    lists = jnp.stack([cell_list, x_list, y_list]).reshape(3, 2, steps, CM, 128)
    lists = lists.transpose(2, 0, 1, 3, 4).reshape(steps, 6 * CM, 128)
    x_conduct = x_coupling[0].astype(F32).reshape(steps, CM, 128)
    y_conduct = y_coupling.astype(F32).reshape(2, steps, CM, 128)
    y_conduct = y_conduct.transpose(1, 0, 2, 3).reshape(steps, 2 * CM, 128)
    last = steps - 1
    x_face, y_face, bottom1, schur1, x_basis1 = pl.pallas_call(
        main_kernel,
        grid=(steps,),
        in_specs=[
            spec((None, 6 * CM, 128), lambda j: (last - j, 0, 0)),
            spec((CM, 128, 256), lambda j: (last - j, 0, 0)),
            spec((CM, 128, 128), lambda j: (last - j, 0, 0)),
            spec((None, CM, 256, 256), lambda j: (1, last - j, 0, 0)),
            spec((None, CM, 256, 128), lambda j: (1, last - j, 0, 0)),
            spec((2, CM, 256, 128), lambda j: (0, last - j, 0, 0)),
            spec((2, CM, 256, 128), lambda j: (0, last - j, 0, 0)),
            spec((None, CM, 128), lambda j: (last - j, 0, 0)),
            spec((None, 2 * CM, 128), lambda j: (last - j, 0, 0)),
        ],
        out_specs=[
            spec((None, CM, 128, 128), lambda j: (0, last - j, 0, 0)),
            spec((2, CM, 128, 128), lambda j: (0, last - j, 0, 0)),
            spec((CM, 128, 128), lambda j: (last - j, 0, 0)),
            spec((CM, 128, 128), lambda j: (last - j, 0, 0)),
            spec((CM, 128, 256), lambda j: (last - j, 0, 0)),
        ],
        out_shape=[
            shape(2, NJ, 128, 128),
            shape(2, NJ, 128, 128),
            shape(NJ, 128, 128),
            shape(NJ, 128, 128),
            shape(NJ, 128, 256),
        ],
        scratch_shapes=[pltpu.VMEM((2, 128, 128), BF16), pltpu.VMEM((2, 128, 128), BF16)],
        compiler_params=PARAMS,
        cost_estimate=cost(4 << 30, 30 << 20),
        name="main",
    )(lists, basis0, schur0, cell_matrix, cell_interp, x_face_interp, y_face_interp, x_conduct, y_conduct)

    end = NJ - 1
    edge_lists = jnp.pad(y_list[:, end], ((0, 6), (0, 0)))
    edge_conduct = jnp.pad(y_coupling[:, end].astype(F32), ((0, 6), (0, 0)))
    y_face = pl.pallas_call(
        edge_kernel,
        grid=(1,),
        in_specs=[
            spec((8, 128), lambda j: (0, 0)),
            spec((None, 128, 128), lambda j: (end, 0, 1)),
            spec((None, 128, 128), lambda j: (end, 0, 0)),
            spec((None, 128, 128), lambda j: (end, 0, 0)),
            spec((None, 128, 128), lambda j: (end, 0, 0)),
            spec((2, 256, 128), lambda j: (0, 0, 0)),
            spec((2, None, 256, 128), lambda j: (0, end, 0, 0)),
            spec((8, 128), lambda j: (0, 0)),
            pl.BlockSpec(memory_space=pl.ANY),
        ],
        out_specs=spec((2, None, 128, 128), lambda j: (0, end, 0, 0)),
        out_shape=shape(2, NJ, 128, 128),
        input_output_aliases={8: 0},
        compiler_params=PARAMS,
        cost_estimate=cost(1 << 27, 1 << 20),
        name="edge",
    )(edge_lists, basis0, bottom1, schur0, schur1, edge_in, y_face_interp, edge_conduct, y_face)

    x_conduct1 = x_coupling[1].astype(F32)
    for first, count, packed_in in ((0, 3, early_in), (3, 1, late_in)):
        x_face = pl.pallas_call(
            last_kernel,
            grid=(count,),
            in_specs=[
                spec((CB, 128, 128), lambda j, first=first: (first + j, 0, 0)),
                spec((CB, 128, 128), lambda j, first=first: (first + j, 0, 0)),
                spec((CB, 128, 256), lambda j, first=first: (first + j, 0, 0)),
                spec((CB, 128), lambda j, first=first: (first + j, 0)),
                spec((CB, 128, 128), lambda j, first=first: (first + j, 0, 0)),
                spec((None, packed, 128), lambda j: (j, 0, 0)),
                pl.BlockSpec(memory_space=pl.ANY),
            ],
            out_specs=spec((None, CB, 128, 128), lambda j, first=first: (1, first + j, 0, 0)),
            out_shape=shape(2, NJ, 128, 128),
            input_output_aliases={6: 0},
            compiler_params=PARAMS,
            cost_estimate=cost(count << 28, count << 21),
            name="last",
        )(bottom1, schur1, x_basis1, x_conduct1, top_in, packed_in, x_face)
    return x_face, y_face


def solution(mesh):
    cells, face, one = P("gx", "yz", None, None), P("gx", "yz", None), P("gx", "yz")
    return jax.shard_map(
        body,
        mesh=mesh,
        in_specs=(cells, face, face, cells, face, one, cells, face, one, cells, face, one),
        out_specs=(cells, cells),
        check_vma=False,
    )
```

time: 126 us -> 71.8 us (0.57)
  the two profiles are of different devices: /device:TPU:90 before, /device:TPU:111 now
where the time goes in v1:
time: 71.8 us; the launch traced here: 71.3 us
  Pallas kernels  54.4 us (76%)
  starting transfers between devices  11.8 us (16%)
  local copies, waits for them, and re-layouts  3.22 us (4%)
  other arithmetic  1.12 us (2%)
  between operations  0.85 us (1%)
    pallas_call x1, Pallas kernels, body(): pl.pallas_call(main_kernel, grid=(steps,), in_specs=[spec((None, 6 * CM,...  31.9 us
    ppermute x4, starting transfers between devices, passed_along(): return lax.ppermute(x, axis, pairs)  11.8 us
    pallas_call x2, Pallas kernels, body(): pl.pallas_call(last_kernel, grid=(count,), in_specs=[spec((CB, 128, 128),...  9.85 us
    pallas_call x1, Pallas kernels, body(): pl.pallas_call(row_schur_kernel, grid=(NJ // CB,), in_specs=[spec((CB, 12...  5.59 us
    pallas_call x1, Pallas kernels, body(): pl.pallas_call(row_basis_kernel, grid=(NJ // CB,), in_specs=[spec((None,...  4.67 us
    unnamed x24, local copies, waits for them, and re-layouts  3.18 us
    pallas_call x1, Pallas kernels, body(): pl.pallas_call(edge_kernel, grid=(1,), in_specs=[spec((8, 128), lambda j:...  2.36 us
  transfers between devices with their start and end apart: 4, of which 0 were waited for; matrix products, arithmetic and copies ran while one was open for 1% of the time, Pallas kernels for 66%

profile of v1, /device:TPU:111, one launch (start us, length us, event | category | flops | bytes accessed | tf_op | source)
XLA Modules:
  0.0 71.3 jit_solution(13835253046115565852)
XLA Ops:
  0.6 0.8 %copy.17 = s32[2,32]{0,1:T(8,128)S(1)} copy(s32[2,32]{1,0:T(2,128)} %param.17) | data formatting | bytes 512 | tf_op args[5]
  1.4 0.9 %fusion = f32[2,32,128]{2,0,1:T(2,128)S(1)} fusion(s32[2,32,128]{2,1,0:T(8,128)} %param.16, s32[2,32]{0,1:T(8,128)S(1)} %copy.17), kind=kLoop, calls=%fused_computation.4 | loop fusion | flops 24576 | bytes 65792 | tf_op jit(solution)/shard_map/convert_element_type | solution.py:217
  2.3 4.7 %row_basis.1 = (bf16[32,128,256]{2,1,0:T(8,128)(2,1)S(1)}, bf16[32,128,128]{2,1,0:T(8,128)(2,1)}) custom-call(f32[2,32,128]{2,1,0:T(8,128)S(1)} %copy.24.list_ref, bf16[2,32,256,128]{3,2,1,0:T(8,128)(2,1)} %interp_ref.6), custom_call_target="tpu_custom_call" | custom-call | flops 16777216 | bytes 5242880 | tf_op jit(solution)/shard_map/row_basis/pallas_call | solution.py:224
  6.9 2.1 %collective-permute-start = (bf16[32,128,128]{2,1,0:T(8,128)(2,1)}, bf16[32,128,128]{2,1,0:T(8,128)(2,1)S(1)}, u32[]{:S(2)}, u32[]{:S(2)}) collective-permute-start(bf16[32,128,128]{2,1,0:T(8,128)(2,1)} %get-tuple-element.18), channel_id=1, source_target_pairs={{8,0},{16,8},{24,16},{32,24},{40,32},{48,40},{56,48},{64,56},{72,6... | collective-permute-start | bytes 3145736 | tf_op jit(solution)/shard_map/ppermute | solution.py:19
  9.0 0.0 copy-start.8
  9.0 0.0 copy-start.9
  9.1 0.0 copy-start.4
  9.1 0.0 copy-start.5
  9.1 5.6 %row_schur.1 = (bf16[32,128,128]{2,1,0:T(8,128)(2,1)S(1)}, bf16[3,528,128]{2,1,0:T(8,128)(2,1)S(1)}, bf16[1,528,128]{2,1,0:T(8,128)(2,1)}, bf16[2,256,128]{2,1,0:T(8,128)(2,1)}) custom-call(bf16[32,128,256]{2,1,0:T(8,128)(2,1)S(1)} %get-tuple-element.13.basis_ref.basis0_ref.bottom0_ref, bf16[2,32,256,256]{3,2,1,0:T(8,128)(2,1)} %matrix_ref.3, ...), custom_call_target="tpu_custom_call" | custom-call | flops 1073741824 | bytes 8388608 | tf_op jit(solution)/shard_map/row_schur/pallas_call | solution.py:240
  14.7 1.0 %copy-done.2 = bf16[32,128,128]{2,1,0:T(8,128)(2,1)} copy-done((bf16[32,128,128]{2,1,0:T(8,128)(2,1)}, bf16[32,128,128]{2,1,0:T(8,128)(2,1)S(1)}, u32[]{:S(2)}) %copy-start.2) | copy-done | bytes 1048600
  15.6 2.9 %collective-permute-start.3 = (bf16[2,256,128]{2,1,0:T(8,128)(2,1)}, bf16[2,256,128]{2,1,0:T(8,128)(2,1)S(1)}, u32[]{:S(2)}, u32[]{:S(2)}) collective-permute-start(bf16[2,256,128]{2,1,0:T(8,128)(2,1)} %get-tuple-element.22), channel_id=1, source_target_pairs={{1,0},{2,1},{3,2},{4,3},{5,4},{6,5},{7,6},{9,8},{10,9},{11,10},{12... | collective-permute-start | bytes 393224 | tf_op jit(solution)/shard_map/ppermute | solution.py:19
  18.5 4.5 %collective-permute-start.1 = (bf16[1,528,128]{2,1,0:T(8,128)(2,1)}, bf16[1,528,128]{2,1,0:T(8,128)(2,1)S(1)}, u32[]{:S(2)}, u32[]{:S(2)}) collective-permute-start(bf16[1,528,128]{2,1,0:T(8,128)(2,1)} %get-tuple-element.19), channel_id=1, source_target_pairs={{8,0},{16,8},{24,16},{32,24},{40,32},{48,40},{56,48},{64,56},{72,6... | collective-permute-start | bytes 405512 | tf_op jit(solution)/shard_map/ppermute | solution.py:19
  23.0 2.4 %collective-permute-start.2 = (bf16[3,528,128]{2,1,0:T(8,128)(2,1)S(1)}, bf16[3,528,128]{2,1,0:T(8,128)(2,1)S(1)}, u32[]{:S(2)}, u32[]{:S(2)}) collective-permute-start(bf16[3,528,128]{2,1,0:T(8,128)(2,1)S(1)} %get-tuple-element.20), channel_id=1, source_target_pairs={{8,0},{16,8},{24,16},{32,24},{40,32},{48,40},{56,48},{64,56},{72,6... | collective-permute-start | bytes 1216520 | tf_op jit(solution)/shard_map/ppermute | solution.py:19
  25.4 0.1 copy.19
  25.5 0.1 copy.21
  25.6 0.1 fusion.1
  25.7 0.1 fusion.2
  25.8 0.1 maximum_bitcast_fusion
  25.9 0.0 copy-start.3
  25.9 1.2 %copy-done.3 = bf16[32,128,128]{2,1,0:T(8,128)(2,1)S(1)} copy-done((bf16[32,128,128]{2,1,0:T(8,128)(2,1)S(1)}, bf16[32,128,128]{2,1,0:T(8,128)(2,1)}, u32[]{:S(2)}) %copy-start.3) | copy-done | bytes 1048600
  27.2 31.9 %main.1 = (bf16[2,32,128,128]{3,2,1,0:T(8,128)(2,1)}, bf16[2,32,128,128]{3,2,1,0:T(8,128)(2,1)}, bf16[32,128,128]{2,1,0:T(8,128)(2,1)S(1)}, bf16[32,128,128]{2,1,0:T(8,128)(2,1)S(1)}, bf16[32,128,256]{2,1,0:T(8,128)(2,1)S(1)}) custom-call(f32[8,24,128]{2,1,0:T(8,128)S(1)} %bitcast.23, bf16[32,128,256]{2,1,0:T(8,128)(2,1)} %copy-done, ...), custom_call_target="tpu_custom_call" | custom-call | flops 4294967296 | bytes 31457280 | tf_op jit(solution)/shard_map/main/pallas_call | solution.py:272
  59.1 2.4 %edge.1 = bf16[2,32,128,128]{3,2,1,0:T(8,128)(2,1)} custom-call(f32[8,128]{1,0:T(8,128)S(1)} %pad.9.list_ref, bf16[32,128,256]{2,1,0:T(8,128)(2,1)S(1)} %copy-done.1, bf16[32,128,128]{2,1,0:T(8,128)(2,1)S(1)} %get-tuple-element.15.bottom_ref.bottom1_ref, bf16[32,128,128]{2,1,0:T(8,128)(2,1)S(1)} %copy-done.3, ...), custom_call_target="tpu_custom_call", output_to_operand_aliasing={{}: (8, {})} | custom-call | flops 134217728 | bytes 1048576 | tf_op jit(solution)/shard_map/edge/pallas_call | solution.py:309
  61.5 7.0 %last.2.face_in = bf16[2,32,128,128]{3,2,1,0:T(8,128)(2,1)} custom-call(bf16[32,128,128]{2,1,0:T(8,128)(2,1)S(1)} %get-tuple-element.15.bottom_ref.bottom1_ref, bf16[32,128,128]{2,1,0:T(8,128)(2,1)S(1)} %get-tuple-element.16.schur_ref.schur1_ref, bf16[32,128,256]{2,1,0:T(8,128)(2,1)S(1)} %get-tuple-element.17.basis_ref, ...), custom_call_target="tpu_custom_call", output_to_operand_aliasing={{}: (6, {})} | custom-call | flops 805306368 | bytes 6291456 | tf_op jit(solution)/shard_map/last/pallas_call | solution.py:333
  68.5 2.8 %last.3 = bf16[2,32,128,128]{3,2,1,0:T(8,128)(2,1)} custom-call(bf16[32,128,128]{2,1,0:T(8,128)(2,1)S(1)} %get-tuple-element.15.bottom_ref.bottom1_ref, bf16[32,128,128]{2,1,0:T(8,128)(2,1)S(1)} %get-tuple-element.16.schur_ref.schur1_ref, bf16[32,128,256]{2,1,0:T(8,128)(2,1)S(1)} %get-tuple-element.17.basis_ref, ...), custom_call_target="tpu_custom_call", output_to_operand_aliasing={{}: (6, {})} | custom-call | flops 268435456 | bytes 2097152 | tf_op jit(solution)/shard_map/last/pallas_call | solution.py:333
  (27 shorter events, 0.1 us)
Async XLA Ops:
  6.9 7.7 %copy-start = (bf16[32,128,256]{2,1,0:T(8,128)(2,1)}, bf16[32,128,256]{2,1,0:T(8,128)(2,1)S(1)}, u32[]{:S(2)}) copy-start(bf16[32,128,256]{2,1,0:T(8,128)(2,1)S(1)} %get-tuple-element.13.basis_ref.basis0_ref.bottom0_ref) | copy-start | bytes 6291460
  6.9 54.6 %collective-permute-start = (bf16[32,128,128]{2,1,0:T(8,128)(2,1)}, bf16[32,128,128]{2,1,0:T(8,128)(2,1)S(1)}, u32[]{:S(2)}, u32[]{:S(2)}) collective-permute-start(bf16[32,128,128]{2,1,0:T(8,128)(2,1)} %get-tuple-element.18), channel_id=1, source_target_pairs={{8,0},{16,8},{24,16},{32,24},{40,32},{48,40},{56,48},{64,56},{72,6... | collective-permute-start | bytes 3145736 | tf_op jit(solution)/shard_map/ppermute | solution.py:19
  9.0 16.4 %copy-start.8 = (s32[2,32]{1,0:T(2,128)S(1)}, s32[2,32]{1,0:T(2,128)}, u32[]{:S(2)}) copy-start(s32[2,32]{1,0:T(2,128)} %param.20) | copy-start | bytes 772
  9.0 16.5 %copy-start.9 = (s32[2,32]{1,0:T(2,128)S(1)}, s32[2,32]{1,0:T(2,128)}, u32[]{:S(2)}) copy-start(s32[2,32]{1,0:T(2,128)} %param.23) | copy-start | bytes 772
  9.0 16.5 %copy-start.7 = (bf16[2,32,128]{2,1,0:T(8,128)(2,1)S(1)}, bf16[2,32,128]{2,1,0:T(8,128)(2,1)}, u32[]{:S(2)}) copy-start(bf16[2,32,128]{2,1,0:T(8,128)(2,1)} %param.13) | copy-start | bytes 49156
  9.0 16.5 %copy-start.6 = (bf16[2,32,128]{2,1,0:T(8,128)(2,1)S(1)}, bf16[2,32,128]{2,1,0:T(8,128)(2,1)}, u32[]{:S(2)}) copy-start(bf16[2,32,128]{2,1,0:T(8,128)(2,1)} %param.14) | copy-start | bytes 49156
  9.1 16.5 %copy-start.4 = (s32[2,32,128]{2,1,0:T(8,128)S(1)}, s32[2,32,128]{2,1,0:T(8,128)}, u32[]{:S(2)}) copy-start(s32[2,32,128]{2,1,0:T(8,128)} %param.19) | copy-start | bytes 98308
  9.1 16.7 %copy-start.5 = (s32[2,32,128]{2,1,0:T(8,128)S(1)}, s32[2,32,128]{2,1,0:T(8,128)}, u32[]{:S(2)}) copy-start(s32[2,32,128]{2,1,0:T(8,128)} %param.22) | copy-start | bytes 98308
  14.7 1.0 %copy-start.2 = (bf16[32,128,128]{2,1,0:T(8,128)(2,1)}, bf16[32,128,128]{2,1,0:T(8,128)(2,1)S(1)}, u32[]{:S(2)}) copy-start(bf16[32,128,128]{2,1,0:T(8,128)(2,1)S(1)} %get-tuple-element.14.schur0_ref) | copy-start | bytes 3145732
  15.6 43.5 %collective-permute-start.3 = (bf16[2,256,128]{2,1,0:T(8,128)(2,1)}, bf16[2,256,128]{2,1,0:T(8,128)(2,1)S(1)}, u32[]{:S(2)}, u32[]{:S(2)}) collective-permute-start(bf16[2,256,128]{2,1,0:T(8,128)(2,1)} %get-tuple-element.22), channel_id=1, source_target_pairs={{1,0},{2,1},{3,2},{4,3},{5,4},{6,5},{7,6},{9,8},{10,9},{11,10},{12... | collective-permute-start | bytes 393224 | tf_op jit(solution)/shard_map/ppermute | solution.py:19
  18.5 50.0 %collective-permute-start.1 = (bf16[1,528,128]{2,1,0:T(8,128)(2,1)}, bf16[1,528,128]{2,1,0:T(8,128)(2,1)S(1)}, u32[]{:S(2)}, u32[]{:S(2)}) collective-permute-start(bf16[1,528,128]{2,1,0:T(8,128)(2,1)} %get-tuple-element.19), channel_id=1, source_target_pairs={{8,0},{16,8},{24,16},{32,24},{40,32},{48,40},{56,48},{64,56},{72,6... | collective-permute-start | bytes 405512 | tf_op jit(solution)/shard_map/ppermute | solution.py:19
  23.0 38.5 %collective-permute-start.2 = (bf16[3,528,128]{2,1,0:T(8,128)(2,1)S(1)}, bf16[3,528,128]{2,1,0:T(8,128)(2,1)S(1)}, u32[]{:S(2)}, u32[]{:S(2)}) collective-permute-start(bf16[3,528,128]{2,1,0:T(8,128)(2,1)S(1)} %get-tuple-element.20), channel_id=1, source_target_pairs={{8,0},{16,8},{24,16},{32,24},{40,32},{48,40},{56,48},{64,56},{72,6... | collective-permute-start | bytes 1216520 | tf_op jit(solution)/shard_map/ppermute | solution.py:19
  25.9 1.2 %copy-start.3 = (bf16[32,128,128]{2,1,0:T(8,128)(2,1)S(1)}, bf16[32,128,128]{2,1,0:T(8,128)(2,1)}, u32[]{:S(2)}) copy-start(bf16[32,128,128]{2,1,0:T(8,128)(2,1)} %copy-done.2) | copy-start | bytes 3145732
  27.2 32.0 %copy-start.1 = (bf16[32,128,256]{2,1,0:T(8,128)(2,1)S(1)}, bf16[32,128,256]{2,1,0:T(8,128)(2,1)}, u32[]{:S(2)}) copy-start(bf16[32,128,256]{2,1,0:T(8,128)(2,1)} %copy-done) | copy-start | bytes 6291460

commit v2 on v0

v2 whole, which is shorter than its diff:
```python
import jax
import jax.numpy as jnp
from jax import lax
from jax.experimental import pallas as pl
from jax.experimental.pallas import tpu as pltpu
from jax.sharding import PartitionSpec as P

F32, BF16 = jnp.float32, jnp.bfloat16
ROWS = (((1,), (1,)), ((), ()))
N = 16


def dot(a, b):
    return jnp.dot(a, b, preferred_element_type=F32).astype(BF16)


def dot_t(a, b):
    return lax.dot_general(a, b, ROWS, preferred_element_type=F32).astype(BF16)


def basis_of(skel, rank, interp, rows):
    one, zero = jnp.ones((), BF16), jnp.zeros((), BF16)
    slots = lax.broadcasted_iota(jnp.int32, (1, 128), 1)
    live = slots < rank
    marked = jnp.where(live, skel, -1).astype(F32).astype(BF16)
    picked = rows == jnp.broadcast_to(marked, (256, 128))
    kept = jnp.where(jnp.broadcast_to(live, (256, 128)), interp, zero)
    turned = jnp.where(picked, one, kept).T
    most = turned[:16]
    for k in range(1, 8):
        most = jnp.maximum(most, turned[16 * k : 16 * k + 16])
    most = jnp.max(most.astype(F32), axis=0, keepdims=True)
    least = jnp.where(most > 0.5, 0.5, -1.0).astype(BF16)
    return jnp.where(turned > jnp.broadcast_to(least, (128, 256)), turned, zero)


def mega(
    matrix_hbm, cell_hbm, x_hbm, y_hbm,
    x_conduct, y_conduct, cell_skel, x_skel, y_skel, cell_rank, x_rank, y_rank,
    x_out, y_out,
    matrix, interp, x_interp, y_interp, tops, bottoms, schurs, x_basis, basis, inner, face,
    x_face, y_face, packed, packed_in, diagonals, diagonals_in,
    in_sem, out_sem, send_sem, recv_sem,
):
    gx, yz = lax.axis_index("gx"), lax.axis_index("yz")
    gxs, yzs = lax.axis_size("gx"), lax.axis_size("yz")
    nj = cell_skel.shape[1]
    groups = nj // N
    has_down, has_up = gx > 0, gx < gxs - 1
    has_left, has_right = yz > 0, yz < yzs - 1

    copies = {}

    def load(name, src, dst):
        copies[name] = pltpu.make_async_copy(src, dst, in_sem.at[len(copies)])
        copies[name].start()

    span = [pl.ds(g * N, N) for g in range(groups)]
    for g in range(groups):
        load(("c", 0, g), cell_hbm.at[0, span[g]], interp.at[0, span[g]])
    for g in range(groups):
        load(("m", 0, g), matrix_hbm.at[0, span[g]], matrix.at[0, span[g]])
    for g in range(groups):
        load(("c", 1, g), cell_hbm.at[1, span[g]], interp.at[1, span[g]])
        load(("m", 1, g), matrix_hbm.at[1, span[g]], matrix.at[1, span[g]])
    for g in range(groups):
        load(("x", 0, g), x_hbm.at[0, span[g]], x_interp.at[0, span[g]])
    for g in range(groups):
        for row in range(2):
            load(("y", row, g), y_hbm.at[row, span[g]], y_interp.at[row, span[g]])
    for g in range(groups):
        load(("x", 1, g), x_hbm.at[1, span[g]], x_interp.at[1, span[g]])

    barrier = pltpu.get_barrier_semaphore()
    for there, device in (
        (has_down, {"gx": gx - 1}),
        (has_up, {"gx": gx + 1}),
        (has_left, {"yz": yz - 1}),
        (has_right, {"yz": yz + 1}),
    ):

        @pl.when(there)
        def _(device=device):
            pl.semaphore_signal(barrier, inc=1, device_id=device, device_id_type=pl.DeviceIdType.MESH)

    unknowns = lax.broadcasted_iota(jnp.int32, (256, 128), 0).astype(F32).astype(BF16)
    down = lax.broadcasted_iota(jnp.int32, (128, 128), 0)
    across = lax.broadcasted_iota(jnp.int32, (128, 128), 1)

    def remote(src, dst, at, device):
        return pltpu.make_async_remote_copy(
            src_ref=src, dst_ref=dst, send_sem=send_sem.at[at], recv_sem=recv_sem.at[at],
            device_id=device, device_id_type=pl.DeviceIdType.MESH,
        )

    top_copy = [
        remote(tops.at[0, span[g]], tops.at[2, span[g]], g, {"gx": gx - 1}) for g in range(groups)
    ]
    half = N // 2
    pack_copy = [
        remote(packed.at[pl.ds(g * half, half)], packed_in.at[pl.ds(g * half, half)], groups + g, {"gx": gx - 1})
        for g in range(groups)
    ]
    line_copy = [remote(diagonals.at[g], diagonals_in.at[g], 2 * groups + g, {"gx": gx - 1}) for g in range(groups)]
    side_copy = [
        remote(ref.at[pl.ds(0, 2), 0], ref.at[pl.ds(0, 2), nj], 3 * groups + k, {"yz": yz - 1})
        for k, ref in enumerate((tops, schurs))
    ]

    def cell_bases(row, g):
        for c in range(N):
            j = g * N + c
            value = basis_of(cell_skel[row, j : j + 1], cell_rank[row, j], interp[row, j], unknowns)
            tops[row, j] = value[:, :128]
            bottoms[row, j] = value[:, 128:]
            basis[c] = value

    def cell_schurs(row, g):
        for c in range(N):
            inner[c] = dot(basis[c], matrix[row, g * N + c])
        for c in range(N):
            schurs[row, g * N + c] = dot_t(inner[c], basis[c])

    def reload(row, g):
        for c in range(N):
            basis[c, :, :128] = tops[row, g * N + c]
            basis[c, :, 128:] = bottoms[row, g * N + c]

    def pack(g):
        lines = []
        for c in range(half):
            j = g * N + 2 * c
            packed[g * half + c] = jnp.where(down <= across, schurs[0, j], schurs[0, j + 1])
            lines.append(
                jnp.sum(jnp.where(down == across, schurs[0, j + 1].astype(F32), 0.0), axis=0, keepdims=True)
            )
        lines.append(jnp.zeros((16 - half, 128), F32))
        diagonals[g] = jnp.concatenate(lines, axis=0).astype(BF16)

    def unpack(g):
        for c in range(half):
            j = g * N + 2 * c
            value = packed_in[g * half + c]
            turned = value.T
            line = jnp.broadcast_to(diagonals_in[g, c : c + 1], (128, 128))
            schurs[2, j] = jnp.where(down <= across, value, turned)
            schurs[2, j + 1] = jnp.where(down == across, line, jnp.where(down > across, value, turned))

    def face_links(row, g, conduct, right):
        for c in range(N):
            j = g * N + c
            scaled = (tops[right(j)].astype(F32) * -conduct[row, j : j + 1].astype(F32)).astype(BF16)
            link = dot_t(bottoms[row, j], scaled)
            face[c, :128, :128] = schurs[row, j]
            face[c, :128, 128:] = link
            face[c, 128:, :128] = link.T

    def face_bases(row, g, skel, rank, values, into, base=0):
        for c in range(N):
            j = g * N + c
            into[base + c] = basis_of(skel[row, j : j + 1], rank[row, j], values[row, j], unknowns)

    def face_ends(row, g, right, bases, out, base=0):
        for c in range(N):
            face[c, 128:, 128:] = schurs[right(g * N + c)]
        for c in range(N):
            inner[c] = dot(bases[base + c], face[c])
        for c in range(N):
            out[row, g * N + c] = dot_t(bases[base + c], inner[c])

    outs = []

    def store(out, hbm, row, g):
        copy = pltpu.make_async_copy(out.at[row, span[g]], hbm.at[row, span[g]], out_sem.at[len(outs)])
        copy.start()
        outs.append(copy)

    count = sum(x.astype(jnp.int32) for x in (has_down, has_up, has_left, has_right))
    for g in range(groups):
        copies["c", 0, g].wait()
        cell_bases(0, g)
        if g == 0:
            pl.semaphore_wait(barrier, count)
        pl.when(has_down)(top_copy[g].start)
    for g in range(groups):
        reload(0, g)
        copies["m", 0, g].wait()
        cell_schurs(0, g)
        pack(g)
        pl.when(has_down)(pack_copy[g].start)
        pl.when(has_down)(line_copy[g].start)
    for g in range(groups):
        copies["c", 1, g].wait()
        cell_bases(1, g)
        copies["m", 1, g].wait()
        cell_schurs(1, g)
        if g == 0:
            for copy in side_copy:
                pl.when(has_left)(copy.start)

    @pl.when(jnp.logical_not(has_right))
    def _():
        for row in range(2):
            tops[row, nj] = jnp.zeros((128, 128), BF16)
            schurs[row, nj] = jnp.zeros((128, 128), BF16)

    @pl.when(jnp.logical_not(has_up))
    def _():
        tops[2] = jnp.zeros(tops.shape[1:], BF16)
        packed_in[...] = jnp.zeros_like(packed_in)
        diagonals_in[...] = jnp.zeros_like(diagonals_in)

    for g in range(groups):
        copies["x", 0, g].wait()
        face_links(0, g, x_conduct, lambda j: (1, j))
        face_bases(0, g, x_skel, x_rank, x_interp, basis)
        face_ends(0, g, lambda j: (1, j), basis, x_face)
        store(x_face, x_out, 0, g)
    for g in range(groups):
        if g == groups - 1:
            for copy in side_copy:
                pl.when(has_right)(copy.wait_recv)
        for row in range(2):
            copies["y", row, g].wait()
            face_links(row, g, y_conduct, lambda j, row=row: (row, j + 1))
            face_bases(row, g, y_skel, y_rank, y_interp, basis)
            face_ends(row, g, lambda j, row=row: (row, j + 1), basis, y_face)
            store(y_face, y_out, row, g)
    for g in range(groups):
        copies["x", 1, g].wait()
        face_bases(1, g, x_skel, x_rank, x_interp, x_basis, g * N)
    for g in range(groups):
        pl.when(has_up)(top_copy[g].wait_recv)
        face_links(1, g, x_conduct, lambda j: (2, j))
        pl.when(has_up)(pack_copy[g].wait_recv)
        pl.when(has_up)(line_copy[g].wait_recv)
        unpack(g)
        face_ends(1, g, lambda j: (2, j), x_basis, x_face, g * N)
        store(x_face, x_out, 1, g)
    for copy in outs:
        copy.wait()
    for copy in top_copy + pack_copy + line_copy:
        pl.when(has_down)(copy.wait_send)
    for copy in side_copy:
        pl.when(has_left)(copy.wait_send)


def body(*args):
    (
        cell_matrix, x_coupling, y_coupling, cell_interp, cell_skel, cell_rank,
        x_face_interp, x_face_skel, x_face_rank, y_face_interp, y_face_skel, y_face_rank,
    ) = args
    nj = cell_skel.shape[1]
    groups = nj // N
    hbm = pl.BlockSpec(memory_space=pl.ANY)
    vmem = pl.BlockSpec(memory_space=pltpu.VMEM)
    smem = pl.BlockSpec(memory_space=pltpu.SMEM)
    out = jax.ShapeDtypeStruct((2, nj, 128, 128), BF16)
    return pl.pallas_call(
        mega,
        in_specs=[hbm] * 4 + [vmem] * 5 + [smem] * 3,
        out_specs=[hbm] * 2,
        out_shape=[out] * 2,
        scratch_shapes=[
            pltpu.VMEM((2, nj, 256, 256), BF16),
            pltpu.VMEM((2, nj, 256, 128), BF16),
            pltpu.VMEM((2, nj, 256, 128), BF16),
            pltpu.VMEM((2, nj, 256, 128), BF16),
            pltpu.VMEM((3, nj + 1, 128, 128), BF16),
            pltpu.VMEM((2, nj, 128, 128), BF16),
            pltpu.VMEM((3, nj + 1, 128, 128), BF16),
            pltpu.VMEM((nj, 128, 256), BF16),
            pltpu.VMEM((N, 128, 256), BF16),
            pltpu.VMEM((N, 128, 256), BF16),
            pltpu.VMEM((N, 256, 256), BF16),
            pltpu.VMEM((2, nj, 128, 128), BF16),
            pltpu.VMEM((2, nj, 128, 128), BF16),
            pltpu.VMEM((nj // 2, 128, 128), BF16),
            pltpu.VMEM((nj // 2, 128, 128), BF16),
            pltpu.VMEM((groups, 16, 128), BF16),
            pltpu.VMEM((groups, 16, 128), BF16),
            pltpu.SemaphoreType.DMA((10 * groups,)),
            pltpu.SemaphoreType.DMA((4 * groups,)),
            pltpu.SemaphoreType.DMA((3 * groups + 2,)),
            pltpu.SemaphoreType.DMA((3 * groups + 2,)),
        ],
        compiler_params=pltpu.CompilerParams(
            collective_id=0, has_side_effects=True, vmem_limit_bytes=60 << 20
        ),
        name="mega",
    )(
        cell_matrix, cell_interp, x_face_interp, y_face_interp,
        x_coupling, y_coupling, cell_skel, x_face_skel, y_face_skel,
        cell_rank, x_face_rank, y_face_rank,
    )


def solution(mesh):
    cells, face, one = P("gx", "yz", None, None), P("gx", "yz", None), P("gx", "yz")
    return jax.shard_map(
        body,
        mesh=mesh,
        in_specs=(cells, face, face, cells, face, one, cells, face, one, cells, face, one),
        out_specs=(cells, cells),
        check_vma=False,
    )
```

time: 126 us -> 46.9 us (0.37); the launches traced: 124 us -> 46.7 us
  matrix products: 44.8 us -> 0 us
  Pallas kernels: 0 us -> 41.4 us
  local copies, waits for them, and re-layouts: 37.8 us -> 4.63 us
  other arithmetic: 17 us -> 0 us
  waiting for transfers between devices: 13.6 us -> 0 us
  starting transfers between devices: 10 us -> 0 us
    dot_general x7 -> x0, matrix products: 44.8 us -> none  [the longest x3 18.9 us: project(): jnp.einsum('...ji,...jk->...ik', left_basis, inner_prod, preferred_elemen...]
    pallas_call x0 -> x1, Pallas kernels: none -> 41.4 us  [body(): pl.pallas_call(mega, in_specs=[hbm] * 4 + [vmem] * 5 + [smem] * 3, out_sp...]
    unnamed x37 -> x4, local copies, waits for them, and re-layouts: 21.1 us -> 4.63 us
    ppermute x4 -> x0, waiting for transfers between devices: 13.6 us -> none  [passed_along(): return lax.ppermute(x, axis, pairs)]
    ppermute x4 -> x0, starting transfers between devices: 10 us -> none  [passed_along(): return lax.ppermute(x, axis, pairs)]
    reduce_or x3 -> x0, other arithmetic: 9.64 us -> none  [make_basis(): kept_rows = jnp.any(picked_rows, axis=-1, keepdims=True)]
    convert_element_type x2 -> x0, local copies, waits for them, and re-layouts: 8.56 us -> none  [the longest x1 4.3 us: body(): coupling_link(x_coupling, cell_basis, right_x_basis).astype(jnp.bfloat16)]
    slice x7 -> x0, local copies, waits for them, and re-layouts: 8.14 us -> none  [the longest x1 4.76 us: body(): right_x_basis = jnp.concatenate([cell_basis[1:], x_basis_in], axis=0)]
  transfers between devices with their start and end apart: 4 -> 0, of which waited for: 2 -> 0; matrix products, arithmetic and copies ran while one was open for 55% -> 0% of each run, Pallas kernels for 0% -> 0%
where the time goes in v2:
time: 46.9 us; the launch traced here: 46.7 us
  Pallas kernels  41.4 us (88%)
  local copies, waits for them, and re-layouts  4.63 us (10%)
  between operations  0.65 us (1%)
    pallas_call x1, Pallas kernels, body(): pl.pallas_call(mega, in_specs=[hbm] * 4 + [vmem] * 5 + [smem] * 3, out_sp...  41.4 us
    unnamed x4, local copies, waits for them, and re-layouts  4.63 us

profile of v2, /device:TPU:90, one launch (start us, length us, event | category | flops | bytes accessed | tf_op | source)
XLA Modules:
  0.0 46.7 jit_solution(11803145423139419802)
XLA Ops:
  0.6 41.4 %mega.1 = (bf16[2,32,128,128]{3,2,1,0:T(8,128)(2,1)}, bf16[2,32,128,128]{3,2,1,0:T(8,128)(2,1)}) custom-call(bf16[2,32,256,256]{3,2,1,0:T(8,128)(2,1)} %matrix_hbm.1, bf16[2,32,256,128]{3,2,1,0:T(8,128)(2,1)} %cell_hbm.1, bf16[2,32,256,128]{3,2,1,0:T(8,128)(2,1)} %x_hbm.1, bf16[2,32,256,128]{3,2,1,0:T(8,128)(2,1)} %y_hbm.1, bf16[2,32,128]{2,1,0:T(8,128)(2,1)} %x_conduct.1, ...), custom_call_target="tpu_custom_call" | custom-call | tf_op jit(solution)/shard_map/mega/pallas_call | solution.py:259
  42.0 0.0 copy-start
  42.0 3.3 %copy.16 = bf16[2,32,128,128]{3,2,1,0:T(8,128)(2,1)} copy(bf16[2,32,128,128]{3,2,1,0:T(8,128)(2,1)} %get-tuple-element.4) | data formatting | bytes 4194304
  45.3 0.0 copy-done
  45.4 1.3 %copy.17 = bf16[2,32,128,128]{3,2,1,0:T(8,128)(2,1)} copy(bf16[2,32,128,128]{3,2,1,0:T(8,128)(2,1)S(1)} %copy-done) | data formatting | bytes 4194304
Async XLA Ops:
  42.0 3.3 %copy-start = (bf16[2,32,128,128]{3,2,1,0:T(8,128)(2,1)S(1)}, bf16[2,32,128,128]{3,2,1,0:T(8,128)(2,1)}, u32[]{:S(2)}) copy-start(bf16[2,32,128,128]{3,2,1,0:T(8,128)(2,1)} %get-tuple-element.5) | copy-start | bytes 6291460

commit v3 on v2

v3 whole, which is shorter than its diff:
```python
import jax
import jax.numpy as jnp
from jax import lax
from jax.experimental import pallas as pl
from jax.experimental.pallas import tpu as pltpu
from jax.sharding import PartitionSpec as P

F32, BF16 = jnp.float32, jnp.bfloat16
ROWS = (((1,), (1,)), ((), ()))
N = 16
CUTS = (0, 10, 18, 26, 32)


def dot(a, b):
    return jnp.dot(a, b, preferred_element_type=F32)


def dot_t(a, b):
    return lax.dot_general(a, b, ROWS, preferred_element_type=F32)


def basis_of(skel, rank, interp, rows):
    one, zero = jnp.ones((), BF16), jnp.zeros((), BF16)
    slots = lax.broadcasted_iota(jnp.int32, (1, 128), 1)
    live = slots < rank
    marked = jnp.where(live, skel, -1).astype(F32).astype(BF16)
    picked = rows == jnp.broadcast_to(marked, (256, 128))
    kept = jnp.where(jnp.broadcast_to(live, (256, 128)), interp, zero)
    turned = jnp.where(picked, one, kept).T
    most = turned[:16]
    for k in range(1, 8):
        most = jnp.maximum(most, turned[16 * k : 16 * k + 16])
    most = jnp.max(most.astype(F32), axis=0, keepdims=True)
    least = jnp.where(most > 0.5, 0.5, -1.0).astype(BF16)
    return jnp.where(turned > jnp.broadcast_to(least, (128, 256)), turned, zero)


def mega(
    matrix_hbm, cell_hbm, x_hbm, y_hbm,
    x_conduct, y_conduct, cell_skel, x_skel, y_skel, cell_rank, x_rank, y_rank,
    x_out, y_out,
    matrix, interp, x_interp, y_interp, tops, bottoms, schurs, x_basis, basis, inner, face,
    x_face, y_face, packed, packed_in, diagonals, diagonals_in, lifted, lifted_in, partial,
    in_sem, out_sem, send_sem, recv_sem,
):
    gx, yz = lax.axis_index("gx"), lax.axis_index("yz")
    gxs, yzs = lax.axis_size("gx"), lax.axis_size("yz")
    nj = cell_skel.shape[1]
    has_down, has_up = gx > 0, gx < gxs - 1
    has_left, has_right = yz > 0, yz < yzs - 1

    ranges = [range(*CUTS[k : k + 2]) for k in range(len(CUTS) - 1)]
    lower, upper = ranges[:2], ranges[2:]
    low = range(lower[0].start, lower[-1].stop)
    high = range(upper[0].start, upper[-1].stop)
    halves = [range(k, k + N) for k in range(0, nj, N)]

    def cut(cols):
        return pl.ds(cols.start, len(cols))

    copies = {}

    def load(kind, row, cols):
        src, dst = {
            "m": (matrix_hbm, matrix), "c": (cell_hbm, interp), "x": (x_hbm, x_interp), "y": (y_hbm, y_interp)
        }[kind]
        copy = pltpu.make_async_copy(src.at[row, cut(cols)], dst.at[row, cut(cols)], in_sem.at[len(copies)])
        copy.start()
        copies[kind, row, cols] = copy

    def loaded(kind, row, cols):
        copies[kind, row, cols].wait()

    for k in range(2):
        load("c", 0, lower[k])
        load("c", 1, upper[k])
        load("x", 1, upper[k])
    load("m", 0, low)
    load("c", 0, high)
    load("m", 0, high)
    load("c", 1, low)
    load("m", 1, low)
    load("m", 1, high)
    for cols in halves:
        load("x", 0, cols)
    for cols in halves:
        load("y", 0, cols)
        load("y", 1, cols)
    load("x", 1, low)

    barrier = pltpu.get_barrier_semaphore()
    for there, device in (
        (has_down, {"gx": gx - 1}),
        (has_up, {"gx": gx + 1}),
        (has_left, {"yz": yz - 1}),
        (has_right, {"yz": yz + 1}),
    ):

        @pl.when(there)
        def _(device=device):
            pl.semaphore_signal(barrier, inc=1, device_id=device, device_id_type=pl.DeviceIdType.MESH)

    unknowns = lax.broadcasted_iota(jnp.int32, (256, 128), 0).astype(F32).astype(BF16)
    down = lax.broadcasted_iota(jnp.int32, (128, 128), 0)
    across = lax.broadcasted_iota(jnp.int32, (128, 128), 1)

    made = []

    def remote(src, dst, device):
        at = len(made)
        made.append(at)
        return pltpu.make_async_remote_copy(
            src_ref=src, dst_ref=dst, send_sem=send_sem.at[at], recv_sem=recv_sem.at[at],
            device_id=device, device_id_type=pl.DeviceIdType.MESH,
        )

    lift = [
        remote(lifted.at[part], lifted_in.at[part], {"gx": gx + 1})
        for part in (pl.ds(cols.start - high.start, len(cols)) for cols in upper)
    ]
    top_copy = [remote(tops.at[0, cut(cols)], tops.at[2, cut(cols)], {"gx": gx - 1}) for cols in lower]
    pack_copy = []
    for k, cols in enumerate(ranges):
        pairs = pl.ds(cols.start // 2, len(cols) // 2)
        pack_copy.append(
            (
                remote(packed.at[pairs], packed_in.at[pairs], {"gx": gx - 1}),
                remote(diagonals.at[k], diagonals_in.at[k], {"gx": gx - 1}),
            )
        )
    side_copy = [
        remote(ref.at[pl.ds(0, 2), 0], ref.at[pl.ds(0, 2), nj], {"yz": yz - 1}) for ref in (tops, schurs)
    ]

    outs = []

    def store(kind, row, cols):
        src, dst = {"x": (x_face, x_out), "y": (y_face, y_out)}[kind]
        copy = pltpu.make_async_copy(src.at[row, cut(cols)], dst.at[row, cut(cols)], out_sem.at[len(outs)])
        copy.start()
        outs.append(copy)

    def cell(row, j):
        return jnp.concatenate([tops[row, j], bottoms[row, j]], axis=1)

    def cell_bases(row, cols):
        for j in cols:
            value = basis_of(cell_skel[row, j : j + 1], cell_rank[row, j], interp[row, j], unknowns)
            tops[row, j] = value[:, :128]
            bottoms[row, j] = value[:, 128:]

    def cell_schurs(row, cols):
        for c, j in enumerate(cols):
            inner[c] = dot(cell(row, j), matrix[row, j]).astype(BF16)
        for c, j in enumerate(cols):
            schurs[row, j] = dot_t(inner[c], cell(row, j)).astype(BF16)

    def pack(k, blocks):
        lines = []
        for c, j in enumerate(range(ranges[k].start, ranges[k].stop, 2)):
            packed[j // 2] = jnp.where(down <= across, blocks(j), blocks(j + 1))
            lines.append(jnp.sum(jnp.where(down == across, blocks(j + 1).astype(F32), 0.0), axis=0, keepdims=True))
        lines.append(jnp.zeros((16 - len(lines), 128), F32))
        diagonals[k] = jnp.concatenate(lines, axis=0).astype(BF16)

    def unpack(k):
        for c, j in enumerate(range(ranges[k].start, ranges[k].stop, 2)):
            value = packed_in[j // 2]
            turned = value.T
            line = jnp.broadcast_to(diagonals_in[k, c : c + 1], (128, 128))
            schurs[2, j] = jnp.where(down <= across, value, turned)
            schurs[2, j + 1] = jnp.where(down == across, line, jnp.where(down > across, value, turned))

    def face_bases(row, cols, skel, rank, values, into):
        for c, j in enumerate(cols):
            into[c] = basis_of(skel[row, j : j + 1], rank[row, j], values[row, j], unknowns)

    def negative(conduct, row, j):
        return -conduct[row, j : j + 1].astype(F32)

    def face_links(row, cols, conduct, right):
        for c, j in enumerate(cols):
            scaled = (tops[right(j)].astype(F32) * negative(conduct, row, j)).astype(BF16)
            link = dot_t(bottoms[row, j], scaled).astype(BF16)
            face[c, :128, :128] = schurs[row, j]
            face[c, :128, 128:] = link
            face[c, 128:, :128] = link.T

    def face_ends(row, cols, right, bases, out, base=0):
        for c, j in enumerate(cols):
            face[base + c, 128:, 128:] = schurs[right(j)]
        for c, j in enumerate(cols):
            inner[c] = dot(bases[base + c], face[base + c]).astype(BF16)
        for c, j in enumerate(cols):
            out[row, j] = dot_t(bases[base + c], inner[c]).astype(BF16)

    def lift_out(cols):
        for j in cols:
            value = basis_of(x_skel[1, j : j + 1], x_rank[1, j], x_interp[1, j], unknowns)
            x_basis[j] = value
            lifted[j - high.start, :, :128] = value[:, 128:]
        for j in cols:
            carried = dot(x_basis[j, :, :128], bottoms[1, j]) * negative(x_conduct, 1, j)
            lifted[j - high.start, :, 128:] = carried.astype(BF16)

    def lift_back(cols):
        for c, j in enumerate(cols):
            both = jnp.concatenate([schurs[0, j], tops[0, j]], axis=1)
            inner[c] = dot(lifted_in[j - high.start, :, :128], both).astype(BF16)
        for c, j in enumerate(cols):
            here = lifted_in[j - high.start]
            value = dot_t(here, inner[c]) + dot_t(inner[c, :, 128:], here[:, 128:])
            face[c, :128, :128] = value.astype(BF16)

    def own_part(cols):
        for c, j in enumerate(cols):
            inner[c, :, :128] = dot(x_basis[j, :, :128], schurs[1, j]).astype(BF16)
        for c, j in enumerate(cols):
            partial[j - high.start] = dot_t(x_basis[j, :, :128], inner[c, :, :128])

    def send(k):
        for copy in pack_copy[k]:
            pl.when(has_down)(copy.start)

    def received(k):
        for copy in pack_copy[k]:
            pl.when(has_up)(copy.wait_recv)

    count = sum(x.astype(jnp.int32) for x in (has_down, has_up, has_left, has_right))
    for k in range(2):
        loaded("c", 0, lower[k])
        cell_bases(0, lower[k])
        if k == 0:
            pl.semaphore_wait(barrier, count)
        pl.when(has_down)(top_copy[k].start)
        loaded("c", 1, upper[k])
        loaded("x", 1, upper[k])
        cell_bases(1, upper[k])
        lift_out(upper[k])
        pl.when(has_up)(lift[k].start)
    loaded("m", 0, low)
    cell_schurs(0, low)
    for k in range(2):
        pack(k, lambda j: schurs[0, j])
        send(k)
    loaded("c", 0, high)
    cell_bases(0, high)
    loaded("m", 0, high)
    cell_schurs(0, high)
    loaded("c", 1, low)
    cell_bases(1, low)
    loaded("m", 1, low)
    cell_schurs(1, low)
    for copy in side_copy:
        pl.when(has_left)(copy.start)
    loaded("m", 1, high)
    cell_schurs(1, high)

    @pl.when(jnp.logical_not(has_right))
    def _():
        for row in range(2):
            tops[row, nj] = jnp.zeros((128, 128), BF16)
            schurs[row, nj] = jnp.zeros((128, 128), BF16)

    @pl.when(jnp.logical_not(has_up))
    def _():
        tops[2] = jnp.zeros(tops.shape[1:], BF16)
        packed_in[...] = jnp.zeros_like(packed_in)
        diagonals_in[...] = jnp.zeros_like(diagonals_in)

    def own_faces(row, cols, kind):
        loaded(kind, row, cols)
        if kind == "x":
            right = lambda j: (1, j)
            face_links(row, cols, x_conduct, right)
            face_bases(row, cols, x_skel, x_rank, x_interp, basis)
            face_ends(row, cols, right, basis, x_face)
        else:
            right = lambda j: (row, j + 1)
            face_links(row, cols, y_conduct, right)
            face_bases(row, cols, y_skel, y_rank, y_interp, basis)
            face_ends(row, cols, right, basis, y_face)
        store(kind, row, cols)

    def answer(k):
        @pl.when(has_down)
        def _():
            lift[k].wait_recv()
            cols = upper[k]
            lift_back(cols)
            pack(2 + k, lambda j: face[j - cols.start, :128, :128])
            for copy in pack_copy[2 + k]:
                copy.start()

    for cols in halves:
        own_faces(0, cols, "x")
    own_faces(0, halves[0], "y")
    own_faces(1, halves[0], "y")
    answer(0)
    for copy in side_copy:
        pl.when(has_right)(copy.wait_recv)
    own_faces(0, halves[1], "y")
    own_faces(1, halves[1], "y")
    own_part(high)
    answer(1)
    loaded("x", 1, low)
    face_bases(1, low, x_skel, x_rank, x_interp, x_basis)
    for copy in top_copy:
        pl.when(has_up)(copy.wait_recv)
    face_links(1, low, x_conduct, lambda j: (2, j))
    for k in range(2):
        received(k)
        unpack(k)
        face_ends(1, lower[k], lambda j: (2, j), x_basis, x_face, lower[k].start)
        store("x", 1, lower[k])
    for k in range(2):
        received(2 + k)
        unpack(2 + k)
        for j in upper[k]:
            x_face[1, j] = (partial[j - high.start] + schurs[2, j].astype(F32)).astype(BF16)
        store("x", 1, upper[k])
    for copy in outs:
        copy.wait()
    for copy in top_copy + [copy for pair in pack_copy for copy in pair]:
        pl.when(has_down)(copy.wait_send)
    for copy in lift:
        pl.when(has_up)(copy.wait_send)
    for copy in side_copy:
        pl.when(has_left)(copy.wait_send)


def finish(x_in, y_in, x_out, y_out, held, in_sem, out_sem):
    rows, columns = x_in.shape[:2]
    pieces = [
        (src.at[row, part], held.at[k, row, part], dst.at[row, part])
        for k, (src, dst) in enumerate(((x_in, x_out), (y_in, y_out)))
        for row in range(rows)
        for part in (pl.ds(at, N) for at in range(0, columns, N))
    ]
    arrive = [pltpu.make_async_copy(src, here, in_sem.at[k]) for k, (src, here, _) in enumerate(pieces)]
    leave = [pltpu.make_async_copy(here, dst, out_sem.at[k]) for k, (_, here, dst) in enumerate(pieces)]
    for copy in arrive:
        copy.start()
    for before, after in zip(arrive, leave):
        before.wait()
        after.start()
    for copy in leave:
        copy.wait()


def body(*args):
    (
        cell_matrix, x_coupling, y_coupling, cell_interp, cell_skel, cell_rank,
        x_face_interp, x_face_skel, x_face_rank, y_face_interp, y_face_skel, y_face_rank,
    ) = args
    nj = cell_skel.shape[1]
    high, most = CUTS[-1] - CUTS[2], max(N, CUTS[2], CUTS[-1] - CUTS[2])
    hbm = pl.BlockSpec(memory_space=pl.ANY)
    vmem = pl.BlockSpec(memory_space=pltpu.VMEM)
    smem = pl.BlockSpec(memory_space=pltpu.SMEM)
    out = jax.ShapeDtypeStruct((2, nj, 128, 128), BF16)
    faces = pl.pallas_call(
        mega,
        in_specs=[hbm] * 4 + [vmem] * 5 + [smem] * 3,
        out_specs=[hbm] * 2,
        out_shape=[out] * 2,
        scratch_shapes=[
            pltpu.VMEM((2, nj, 256, 256), BF16),
            pltpu.VMEM((2, nj, 256, 128), BF16),
            pltpu.VMEM((2, nj, 256, 128), BF16),
            pltpu.VMEM((2, nj, 256, 128), BF16),
            pltpu.VMEM((3, nj + 1, 128, 128), BF16),
            pltpu.VMEM((2, nj, 128, 128), BF16),
            pltpu.VMEM((3, nj + 1, 128, 128), BF16),
            pltpu.VMEM((nj, 128, 256), BF16),
            pltpu.VMEM((N, 128, 256), BF16),
            pltpu.VMEM((most, 128, 256), BF16),
            pltpu.VMEM((most, 256, 256), BF16),
            pltpu.VMEM((2, nj, 128, 128), BF16),
            pltpu.VMEM((2, nj, 128, 128), BF16),
            pltpu.VMEM((nj // 2, 128, 128), BF16),
            pltpu.VMEM((nj // 2, 128, 128), BF16),
            pltpu.VMEM((4, 16, 128), BF16),
            pltpu.VMEM((4, 16, 128), BF16),
            pltpu.VMEM((high, 128, 256), BF16),
            pltpu.VMEM((high, 128, 256), BF16),
            pltpu.VMEM((high, 128, 128), F32),
            pltpu.SemaphoreType.DMA((19,)),
            pltpu.SemaphoreType.DMA((10,)),
            pltpu.SemaphoreType.DMA((14,)),
            pltpu.SemaphoreType.DMA((14,)),
        ],
        compiler_params=pltpu.CompilerParams(
            collective_id=0, has_side_effects=True, vmem_limit_bytes=60 << 20
        ),
        name="mega",
    )(
        cell_matrix, cell_interp, x_face_interp, y_face_interp,
        x_coupling, y_coupling, cell_skel, x_face_skel, y_face_skel,
        cell_rank, x_face_rank, y_face_rank,
    )
    return pl.pallas_call(
        finish,
        in_specs=[hbm] * 2,
        out_specs=[hbm] * 2,
        out_shape=[out] * 2,
        scratch_shapes=[
            pltpu.VMEM((2, 2, nj, 128, 128), BF16),
            pltpu.SemaphoreType.DMA((4 * nj // N,)),
            pltpu.SemaphoreType.DMA((4 * nj // N,)),
        ],
        compiler_params=pltpu.CompilerParams(vmem_limit_bytes=60 << 20),
        name="finish",
    )(*faces)


def solution(mesh):
    cells, face, one = P("gx", "yz", None, None), P("gx", "yz", None), P("gx", "yz")
    return jax.shard_map(
        body,
        mesh=mesh,
        in_specs=(cells, face, face, cells, face, one, cells, face, one, cells, face, one),
        out_specs=(cells, cells),
        check_vma=False,
    )
```

time: 46.9 us -> 37 us (0.79)
  Pallas kernels: 41.4 us -> 36 us
  local copies, waits for them, and re-layouts: 4.63 us -> 0 us
    pallas_call x1, Pallas kernels: 41.4 us -> 32.4 us  [body(): pl.pallas_call(mega, in_specs=[hbm] * 4 + [vmem] * 5 + [smem] * 3, out_sp...]
    unnamed x4 -> x0, local copies, waits for them, and re-layouts: 4.63 us -> none
    pallas_call x0 -> x1, Pallas kernels: none -> 3.58 us  [body(): pl.pallas_call(finish, in_specs=[hbm] * 2, out_specs=[hbm] * 2, out_shape...]
where the time goes in v3:
time: 37 us; the launch traced here: 36.8 us
  Pallas kernels  36 us (97%)
  between operations  0.8 us (2%)
    pallas_call x1, Pallas kernels, body(): pl.pallas_call(mega, in_specs=[hbm] * 4 + [vmem] * 5 + [smem] * 3, out_sp...  32.4 us
    pallas_call x1, Pallas kernels, body(): pl.pallas_call(finish, in_specs=[hbm] * 2, out_specs=[hbm] * 2, out_shape...  3.58 us

profile of v3, /device:TPU:90, one launch (start us, length us, event | category | flops | bytes accessed | tf_op | source)
XLA Modules:
  0.0 36.8 jit_solution(10008634408704055393)
XLA Ops:
  0.6 32.4 %mega.1 = (bf16[2,32,128,128]{3,2,1,0:T(8,128)(2,1)}, bf16[2,32,128,128]{3,2,1,0:T(8,128)(2,1)}) custom-call(bf16[2,32,256,256]{3,2,1,0:T(8,128)(2,1)} %matrix_hbm.1, bf16[2,32,256,128]{3,2,1,0:T(8,128)(2,1)} %cell_hbm.1, bf16[2,32,256,128]{3,2,1,0:T(8,128)(2,1)} %x_hbm.1, bf16[2,32,256,128]{3,2,1,0:T(8,128)(2,1)} %y_hbm.1, bf16[2,32,128]{2,1,0:T(8,128)(2,1)} %x_conduct.1, ...), custom_call_target="tpu_custom_call" | custom-call | tf_op jit(solution)/shard_map/mega/pallas_call | solution.py:362
  33.1 3.6 %finish.1 = (bf16[2,32,128,128]{3,2,1,0:T(8,128)(2,1)}, bf16[2,32,128,128]{3,2,1,0:T(8,128)(2,1)}) custom-call(bf16[2,32,128,128]{3,2,1,0:T(8,128)(2,1)} %get-tuple-element.4.x_in, bf16[2,32,128,128]{3,2,1,0:T(8,128)(2,1)} %get-tuple-element.5.y_in), custom_call_target="tpu_custom_call" | custom-call | tf_op jit(solution)/shard_map/finish/pallas_call | solution.py:402

commit v4 on v3

--- a/solution.py
+++ b/solution.py
@@ -8,7 +8,8 @@
 F32, BF16 = jnp.float32, jnp.bfloat16
 ROWS = (((1,), (1,)), ((), ()))
 N = 16
-CUTS = (0, 10, 18, 26, 32)
+LOWER = ((0, 6), (6, 18))
+UPPER = ((18, 22), (22, 28), (28, 32))
 
 
 def dot(a, b):
@@ -49,8 +50,8 @@
     has_down, has_up = gx > 0, gx < gxs - 1
     has_left, has_right = yz > 0, yz < yzs - 1
 
-    ranges = [range(*CUTS[k : k + 2]) for k in range(len(CUTS) - 1)]
-    lower, upper = ranges[:2], ranges[2:]
+    lower, upper = [range(*ends) for ends in LOWER], [range(*ends) for ends in UPPER]
+    ranges = lower + upper
     low = range(lower[0].start, lower[-1].stop)
     high = range(upper[0].start, upper[-1].stop)
     halves = [range(k, k + N) for k in range(0, nj, N)]
@@ -71,10 +72,11 @@
     def loaded(kind, row, cols):
         copies[kind, row, cols].wait()
 
-    for k in range(2):
-        load("c", 0, lower[k])
-        load("c", 1, upper[k])
-        load("x", 1, upper[k])
+    for k, cols in enumerate(upper):
+        load("c", 1, cols)
+        load("x", 1, cols)
+        if k < len(lower):
+            load("c", 0, lower[k])
     load("m", 0, low)
     load("c", 0, high)
     load("m", 0, high)
@@ -227,20 +229,21 @@
             pl.when(has_up)(copy.wait_recv)
 
     count = sum(x.astype(jnp.int32) for x in (has_down, has_up, has_left, has_right))
-    for k in range(2):
-        loaded("c", 0, lower[k])
-        cell_bases(0, lower[k])
+    for k, cols in enumerate(upper):
+        loaded("c", 1, cols)
+        loaded("x", 1, cols)
+        cell_bases(1, cols)
+        lift_out(cols)
         if k == 0:
             pl.semaphore_wait(barrier, count)
-        pl.when(has_down)(top_copy[k].start)
-        loaded("c", 1, upper[k])
-        loaded("x", 1, upper[k])
-        cell_bases(1, upper[k])
-        lift_out(upper[k])
         pl.when(has_up)(lift[k].start)
+        if k < len(lower):
+            loaded("c", 0, lower[k])
+            cell_bases(0, lower[k])
+            pl.when(has_down)(top_copy[k].start)
     loaded("m", 0, low)
     cell_schurs(0, low)
-    for k in range(2):
+    for k in range(len(lower)):
         pack(k, lambda j: schurs[0, j])
         send(k)
     loaded("c", 0, high)
@@ -288,8 +291,8 @@
             lift[k].wait_recv()
             cols = upper[k]
             lift_back(cols)
-            pack(2 + k, lambda j: face[j - cols.start, :128, :128])
-            for copy in pack_copy[2 + k]:
+            pack(len(lower) + k, lambda j: face[j - cols.start, :128, :128])
+            for copy in pack_copy[len(lower) + k]:
                 copy.start()
 
     for cols in halves:
@@ -301,24 +304,25 @@
         pl.when(has_right)(copy.wait_recv)
     own_faces(0, halves[1], "y")
     own_faces(1, halves[1], "y")
+    answer(1)
     own_part(high)
-    answer(1)
     loaded("x", 1, low)
     face_bases(1, low, x_skel, x_rank, x_interp, x_basis)
     for copy in top_copy:
         pl.when(has_up)(copy.wait_recv)
     face_links(1, low, x_conduct, lambda j: (2, j))
-    for k in range(2):
+    for k, cols in enumerate(lower):
         received(k)
         unpack(k)
-        face_ends(1, lower[k], lambda j: (2, j), x_basis, x_face, lower[k].start)
-        store("x", 1, lower[k])
-    for k in range(2):
-        received(2 + k)
-        unpack(2 + k)
-        for j in upper[k]:
+        face_ends(1, cols, lambda j: (2, j), x_basis, x_face, cols.start)
+        store("x", 1, cols)
+    answer(2)
+    for k, cols in enumerate(upper, len(lower)):
+        received(k)
+        unpack(k)
+        for j in cols:
             x_face[1, j] = (partial[j - high.start] + schurs[2, j].astype(F32)).astype(BF16)
-        store("x", 1, upper[k])
+        store("x", 1, cols)
     for copy in outs:
         copy.wait()
     for copy in top_copy + [copy for pair in pack_copy for copy in pair]:
@@ -330,12 +334,10 @@
 
 
 def finish(x_in, y_in, x_out, y_out, held, in_sem, out_sem):
-    rows, columns = x_in.shape[:2]
     pieces = [
-        (src.at[row, part], held.at[k, row, part], dst.at[row, part])
+        (src.at[row], held.at[k, row], dst.at[row])
         for k, (src, dst) in enumerate(((x_in, x_out), (y_in, y_out)))
-        for row in range(rows)
-        for part in (pl.ds(at, N) for at in range(0, columns, N))
+        for row in range(x_in.shape[0])
     ]
     arrive = [pltpu.make_async_copy(src, here, in_sem.at[k]) for k, (src, here, _) in enumerate(pieces)]
     leave = [pltpu.make_async_copy(here, dst, out_sem.at[k]) for k, (_, here, dst) in enumerate(pieces)]
@@ -354,7 +356,8 @@
         x_face_interp, x_face_skel, x_face_rank, y_face_interp, y_face_skel, y_face_rank,
     ) = args
     nj = cell_skel.shape[1]
-    high, most = CUTS[-1] - CUTS[2], max(N, CUTS[2], CUTS[-1] - CUTS[2])
+    low, high = LOWER[-1][1] - LOWER[0][0], UPPER[-1][1] - UPPER[0][0]
+    most = max(N, low, high)
     hbm = pl.BlockSpec(memory_space=pl.ANY)
     vmem = pl.BlockSpec(memory_space=pltpu.VMEM)
     smem = pl.BlockSpec(memory_space=pltpu.SMEM)
@@ -380,15 +383,15 @@
             pltpu.VMEM((2, nj, 128, 128), BF16),
             pltpu.VMEM((nj // 2, 128, 128), BF16),
             pltpu.VMEM((nj // 2, 128, 128), BF16),
-            pltpu.VMEM((4, 16, 128), BF16),
-            pltpu.VMEM((4, 16, 128), BF16),
+            pltpu.VMEM((len(LOWER + UPPER), 16, 128), BF16),
+            pltpu.VMEM((len(LOWER + UPPER), 16, 128), BF16),
             pltpu.VMEM((high, 128, 256), BF16),
             pltpu.VMEM((high, 128, 256), BF16),
             pltpu.VMEM((high, 128, 128), F32),
-            pltpu.SemaphoreType.DMA((19,)),
-            pltpu.SemaphoreType.DMA((10,)),
-            pltpu.SemaphoreType.DMA((14,)),
-            pltpu.SemaphoreType.DMA((14,)),
+            pltpu.SemaphoreType.DMA((21,)),
+            pltpu.SemaphoreType.DMA((11,)),
+            pltpu.SemaphoreType.DMA((17,)),
+            pltpu.SemaphoreType.DMA((17,)),
         ],
         compiler_params=pltpu.CompilerParams(
             collective_id=0, has_side_effects=True, vmem_limit_bytes=60 << 20
@@ -406,8 +409,8 @@
         out_shape=[out] * 2,
         scratch_shapes=[
             pltpu.VMEM((2, 2, nj, 128, 128), BF16),
-            pltpu.SemaphoreType.DMA((4 * nj // N,)),
-            pltpu.SemaphoreType.DMA((4 * nj // N,)),
+            pltpu.SemaphoreType.DMA((4,)),
+            pltpu.SemaphoreType.DMA((4,)),
         ],
         compiler_params=pltpu.CompilerParams(vmem_limit_bytes=60 << 20),
         name="finish",

time: 37 us -> 36.3 us (0.981)
  the two profiles are of different devices: /device:TPU:90 before, /device:TPU:22 now
where the time goes in v4:
time: 36.3 us; the launch traced here: 36.1 us
  Pallas kernels  35.3 us (97%)
  between operations  0.8 us (2%)
    pallas_call x1, Pallas kernels, body(): pl.pallas_call(mega, in_specs=[hbm] * 4 + [vmem] * 5 + [smem] * 3, out_sp...  32 us
    pallas_call x1, Pallas kernels, body(): pl.pallas_call(finish, in_specs=[hbm] * 2, out_specs=[hbm] * 2, out_shape...  3.3 us

profile of v4, /device:TPU:22, one launch (start us, length us, event | category | flops | bytes accessed | tf_op | source)
XLA Modules:
  0.0 36.1 jit_solution(10178600695442657973)
XLA Ops:
  0.6 32.0 %mega.1 = (bf16[2,32,128,128]{3,2,1,0:T(8,128)(2,1)}, bf16[2,32,128,128]{3,2,1,0:T(8,128)(2,1)}) custom-call(bf16[2,32,256,256]{3,2,1,0:T(8,128)(2,1)} %matrix_hbm.1, bf16[2,32,256,128]{3,2,1,0:T(8,128)(2,1)} %cell_hbm.1, bf16[2,32,256,128]{3,2,1,0:T(8,128)(2,1)} %x_hbm.1, bf16[2,32,256,128]{3,2,1,0:T(8,128)(2,1)} %y_hbm.1, bf16[2,32,128]{2,1,0:T(8,128)(2,1)} %x_conduct.1, ...), custom_call_target="tpu_custom_call" | custom-call | tf_op jit(solution)/shard_map/mega/pallas_call | solution.py:365
  32.7 3.3 %finish.1 = (bf16[2,32,128,128]{3,2,1,0:T(8,128)(2,1)}, bf16[2,32,128,128]{3,2,1,0:T(8,128)(2,1)}) custom-call(bf16[2,32,128,128]{3,2,1,0:T(8,128)(2,1)} %get-tuple-element.4.x_in, bf16[2,32,128,128]{3,2,1,0:T(8,128)(2,1)} %get-tuple-element.5.y_in), custom_call_target="tpu_custom_call" | custom-call | tf_op jit(solution)/shard_map/finish/pallas_call | solution.py:405

commit v5 on v4

--- a/solution.py
+++ b/solution.py
@@ -8,7 +8,7 @@
 F32, BF16 = jnp.float32, jnp.bfloat16
 ROWS = (((1,), (1,)), ((), ()))
 N = 16
-LOWER = ((0, 6), (6, 18))
+LOWER = ((0, 4), (4, 18))
 UPPER = ((18, 22), (22, 28), (28, 32))
 
 
@@ -73,10 +73,10 @@
         copies[kind, row, cols].wait()
 
     for k, cols in enumerate(upper):
+        if k < len(lower):
+            load("c", 0, lower[k])
         load("c", 1, cols)
         load("x", 1, cols)
-        if k < len(lower):
-            load("c", 0, lower[k])
     load("m", 0, low)
     load("c", 0, high)
     load("m", 0, high)
@@ -230,17 +230,17 @@
 
     count = sum(x.astype(jnp.int32) for x in (has_down, has_up, has_left, has_right))
     for k, cols in enumerate(upper):
+        if k < len(lower):
+            loaded("c", 0, lower[k])
+            cell_bases(0, lower[k])
+            if k == 0:
+                pl.semaphore_wait(barrier, count)
+            pl.when(has_down)(top_copy[k].start)
         loaded("c", 1, cols)
         loaded("x", 1, cols)
         cell_bases(1, cols)
         lift_out(cols)
-        if k == 0:
-            pl.semaphore_wait(barrier, count)
         pl.when(has_up)(lift[k].start)
-        if k < len(lower):
-            loaded("c", 0, lower[k])
-            cell_bases(0, lower[k])
-            pl.when(has_down)(top_copy[k].start)
     loaded("m", 0, low)
     cell_schurs(0, low)
     for k in range(len(lower)):

time: 36.3 us -> 36.2 us (level)
  the two profiles are of different devices: /device:TPU:22 before, /device:TPU:90 now
where the time goes in v5:
time: 36.2 us; the launch traced here: 35.8 us
  Pallas kernels  35 us (97%)
  between operations  0.8 us (2%)
    pallas_call x1, Pallas kernels, body(): pl.pallas_call(mega, in_specs=[hbm] * 4 + [vmem] * 5 + [smem] * 3, out_sp...  31.7 us
    pallas_call x1, Pallas kernels, body(): pl.pallas_call(finish, in_specs=[hbm] * 2, out_specs=[hbm] * 2, out_shape...  3.3 us

profile of v5, /device:TPU:90, one launch (start us, length us, event | category | flops | bytes accessed | tf_op | source)
XLA Modules:
  0.0 35.8 jit_solution(10372454178392114428)
XLA Ops:
  0.6 31.7 %mega.1 = (bf16[2,32,128,128]{3,2,1,0:T(8,128)(2,1)}, bf16[2,32,128,128]{3,2,1,0:T(8,128)(2,1)}) custom-call(bf16[2,32,256,256]{3,2,1,0:T(8,128)(2,1)} %matrix_hbm.1, bf16[2,32,256,128]{3,2,1,0:T(8,128)(2,1)} %cell_hbm.1, bf16[2,32,256,128]{3,2,1,0:T(8,128)(2,1)} %x_hbm.1, bf16[2,32,256,128]{3,2,1,0:T(8,128)(2,1)} %y_hbm.1, bf16[2,32,128]{2,1,0:T(8,128)(2,1)} %x_conduct.1, ...), custom_call_target="tpu_custom_call" | custom-call | tf_op jit(solution)/shard_map/mega/pallas_call | solution.py:365
  32.3 3.3 %finish.1 = (bf16[2,32,128,128]{3,2,1,0:T(8,128)(2,1)}, bf16[2,32,128,128]{3,2,1,0:T(8,128)(2,1)}) custom-call(bf16[2,32,128,128]{3,2,1,0:T(8,128)(2,1)} %get-tuple-element.4.x_in, bf16[2,32,128,128]{3,2,1,0:T(8,128)(2,1)} %get-tuple-element.5.y_in), custom_call_target="tpu_custom_call" | custom-call | tf_op jit(solution)/shard_map/finish/pallas_call | solution.py:405

commit v6 on v5

--- a/solution.py
+++ b/solution.py
@@ -39,10 +39,10 @@
 def mega(
     matrix_hbm, cell_hbm, x_hbm, y_hbm,
     x_conduct, y_conduct, cell_skel, x_skel, y_skel, cell_rank, x_rank, y_rank,
-    x_out, y_out,
+    x_out, y_out, late_packed, late_lines, late_part,
     matrix, interp, x_interp, y_interp, tops, bottoms, schurs, x_basis, basis, inner, face,
     x_face, y_face, packed, packed_in, diagonals, diagonals_in, lifted, lifted_in, partial,
-    in_sem, out_sem, send_sem, recv_sem,
+    late_sem, in_sem, out_sem, send_sem, recv_sem,
 ):
     gx, yz = lax.axis_index("gx"), lax.axis_index("yz")
     gxs, yzs = lax.axis_size("gx"), lax.axis_size("yz")
@@ -58,6 +58,18 @@
 
     def cut(cols):
         return pl.ds(cols.start, len(cols))
+
+    barrier = pltpu.get_barrier_semaphore()
+    for there, device in (
+        (has_down, {"gx": gx - 1}),
+        (has_up, {"gx": gx + 1}),
+        (has_left, {"yz": yz - 1}),
+        (has_right, {"yz": yz + 1}),
+    ):
+
+        @pl.when(there)
+        def _(device=device):
+            pl.semaphore_signal(barrier, inc=1, device_id=device, device_id_type=pl.DeviceIdType.MESH)
 
     copies = {}
 
@@ -90,18 +102,6 @@
         load("y", 1, cols)
     load("x", 1, low)
 
-    barrier = pltpu.get_barrier_semaphore()
-    for there, device in (
-        (has_down, {"gx": gx - 1}),
-        (has_up, {"gx": gx + 1}),
-        (has_left, {"yz": yz - 1}),
-        (has_right, {"yz": yz + 1}),
-    ):
-
-        @pl.when(there)
-        def _(device=device):
-            pl.semaphore_signal(barrier, inc=1, device_id=device, device_id_type=pl.DeviceIdType.MESH)
-
     unknowns = lax.broadcasted_iota(jnp.int32, (256, 128), 0).astype(F32).astype(BF16)
     down = lax.broadcasted_iota(jnp.int32, (128, 128), 0)
     across = lax.broadcasted_iota(jnp.int32, (128, 128), 1)
@@ -124,10 +124,11 @@
     pack_copy = []
     for k, cols in enumerate(ranges):
         pairs = pl.ds(cols.start // 2, len(cols) // 2)
+        late = cols is upper[-1]
         pack_copy.append(
             (
-                remote(packed.at[pairs], packed_in.at[pairs], {"gx": gx - 1}),
-                remote(diagonals.at[k], diagonals_in.at[k], {"gx": gx - 1}),
+                remote(packed.at[pairs], late_packed if late else packed_in.at[pairs], {"gx": gx - 1}),
+                remote(diagonals.at[k], late_lines if late else diagonals_in.at[k], {"gx": gx - 1}),
             )
         )
     side_copy = [
@@ -311,18 +312,36 @@
     for copy in top_copy:
         pl.when(has_up)(copy.wait_recv)
     face_links(1, low, x_conduct, lambda j: (2, j))
+    last = pl.ds(upper[-1].start - high.start, len(upper[-1]))
+    part_copy = pltpu.make_async_copy(partial.at[last], late_part, late_sem.at[0])
+    part_copy.start()
+    fill = [
+        pltpu.make_async_copy(packed_in.at[pl.ds(0, len(upper[-1]) // 2)], late_packed, late_sem.at[1]),
+        pltpu.make_async_copy(diagonals_in.at[0], late_lines, late_sem.at[2]),
+    ]
+
+    @pl.when(jnp.logical_not(has_up))
+    def _():
+        for copy in fill:
+            copy.start()
+        for copy in fill:
+            copy.wait()
+
     for k, cols in enumerate(lower):
+        if k == len(lower) - 1:
+            answer(len(upper) - 1)
         received(k)
         unpack(k)
         face_ends(1, cols, lambda j: (2, j), x_basis, x_face, cols.start)
         store("x", 1, cols)
-    answer(2)
-    for k, cols in enumerate(upper, len(lower)):
+    for k, cols in enumerate(upper[:-1], len(lower)):
         received(k)
         unpack(k)
         for j in cols:
             x_face[1, j] = (partial[j - high.start] + schurs[2, j].astype(F32)).astype(BF16)
         store("x", 1, cols)
+    part_copy.wait()
+    received(len(ranges) - 1)
     for copy in outs:
         copy.wait()
     for copy in top_copy + [copy for pair in pack_copy for copy in pair]:
@@ -333,19 +352,38 @@
         pl.when(has_left)(copy.wait_send)
 
 
-def finish(x_in, y_in, x_out, y_out, held, in_sem, out_sem):
+def finish(x_in, y_in, packed_in, lines_in, part_in, x_out, y_out, held, packed, lines, part, in_sem, out_sem):
+    first, stop = UPPER[-1]
+    early, late = pl.ds(0, first), pl.ds(first, stop - first)
     pieces = [
-        (src.at[row], held.at[k, row], dst.at[row])
-        for k, (src, dst) in enumerate(((x_in, x_out), (y_in, y_out)))
-        for row in range(x_in.shape[0])
+        (y_in.at[0], held.at[1, 0], y_out.at[0]),
+        (y_in.at[1], held.at[1, 1], y_out.at[1]),
+        (x_in.at[0], held.at[0, 0], x_out.at[0]),
+        (x_in.at[1, early], held.at[0, 1, early], x_out.at[1, early]),
     ]
     arrive = [pltpu.make_async_copy(src, here, in_sem.at[k]) for k, (src, here, _) in enumerate(pieces)]
     leave = [pltpu.make_async_copy(here, dst, out_sem.at[k]) for k, (_, here, dst) in enumerate(pieces)]
+    for src, here in ((packed_in, packed), (lines_in, lines), (part_in, part)):
+        arrive.append(pltpu.make_async_copy(src, here, in_sem.at[len(arrive)]))
     for copy in arrive:
         copy.start()
     for before, after in zip(arrive, leave):
         before.wait()
         after.start()
+    for copy in arrive[len(leave) :]:
+        copy.wait()
+    down = lax.broadcasted_iota(jnp.int32, (128, 128), 0)
+    across = lax.broadcasted_iota(jnp.int32, (128, 128), 1)
+    for c in range((stop - first) // 2):
+        value = packed[c]
+        turned = value.T
+        line = jnp.broadcast_to(lines[c : c + 1], (128, 128))
+        one = jnp.where(down <= across, value, turned)
+        two = jnp.where(down == across, line, jnp.where(down > across, value, turned))
+        for k, answer in ((2 * c, one), (2 * c + 1, two)):
+            held[0, 1, first + k] = (part[k] + answer.astype(F32)).astype(BF16)
+    leave.append(pltpu.make_async_copy(held.at[0, 1, late], x_out.at[1, late], out_sem.at[len(leave)]))
+    leave[-1].start()
     for copy in leave:
         copy.wait()
 
@@ -362,11 +400,17 @@
     vmem = pl.BlockSpec(memory_space=pltpu.VMEM)
     smem = pl.BlockSpec(memory_space=pltpu.SMEM)
     out = jax.ShapeDtypeStruct((2, nj, 128, 128), BF16)
+    count = UPPER[-1][1] - UPPER[-1][0]
+    late = [
+        jax.ShapeDtypeStruct((count // 2, 128, 128), BF16),
+        jax.ShapeDtypeStruct((16, 128), BF16),
+        jax.ShapeDtypeStruct((count, 128, 128), F32),
+    ]
     faces = pl.pallas_call(
         mega,
         in_specs=[hbm] * 4 + [vmem] * 5 + [smem] * 3,
-        out_specs=[hbm] * 2,
-        out_shape=[out] * 2,
+        out_specs=[hbm] * 5,
+        out_shape=[out] * 2 + late,
         scratch_shapes=[
             pltpu.VMEM((2, nj, 256, 256), BF16),
             pltpu.VMEM((2, nj, 256, 128), BF16),
@@ -388,8 +432,9 @@
             pltpu.VMEM((high, 128, 256), BF16),
             pltpu.VMEM((high, 128, 256), BF16),
             pltpu.VMEM((high, 128, 128), F32),
+            pltpu.SemaphoreType.DMA((3,)),
             pltpu.SemaphoreType.DMA((21,)),
-            pltpu.SemaphoreType.DMA((11,)),
+            pltpu.SemaphoreType.DMA((10,)),
             pltpu.SemaphoreType.DMA((17,)),
             pltpu.SemaphoreType.DMA((17,)),
         ],
@@ -404,13 +449,16 @@
     )
     return pl.pallas_call(
         finish,
-        in_specs=[hbm] * 2,
+        in_specs=[hbm] * 5,
         out_specs=[hbm] * 2,
         out_shape=[out] * 2,
         scratch_shapes=[
             pltpu.VMEM((2, 2, nj, 128, 128), BF16),
-            pltpu.SemaphoreType.DMA((4,)),
-            pltpu.SemaphoreType.DMA((4,)),
+            pltpu.VMEM(late[0].shape, BF16),
+            pltpu.VMEM(late[1].shape, BF16),
+            pltpu.VMEM(late[2].shape, F32),
+            pltpu.SemaphoreType.DMA((7,)),
+            pltpu.SemaphoreType.DMA((5,)),
         ],
         compiler_params=pltpu.CompilerParams(vmem_limit_bytes=60 << 20),
         name="finish",

time: 36.2 us -> 35.3 us (0.975)
  Pallas kernels: 35 us -> 34.3 us
    pallas_call x1, Pallas kernels: 31.7 us -> 31 us  [body(): pl.pallas_call(mega, in_specs=[hbm] * 4 + [vmem] * 5 + [smem] * 3, out_sp...]
where the time goes in v6:
time: 35.3 us; the launch traced here: 35.1 us
  Pallas kernels  34.3 us (97%)
  between operations  0.8 us (2%)
    pallas_call x1, Pallas kernels, body(): pl.pallas_call(mega, in_specs=[hbm] * 4 + [vmem] * 5 + [smem] * 3, out_sp...  31 us
    pallas_call x1, Pallas kernels, body(): pl.pallas_call(finish, in_specs=[hbm] * 5, out_specs=[hbm] * 2, out_shape...  3.32 us

profile of v6, /device:TPU:90, one launch (start us, length us, event | category | flops | bytes accessed | tf_op | source)
XLA Modules:
  0.0 35.1 jit_solution(9857568945715528251)
XLA Ops:
  0.6 31.0 %mega.1 = (bf16[2,32,128,128]{3,2,1,0:T(8,128)(2,1)}, bf16[2,32,128,128]{3,2,1,0:T(8,128)(2,1)}, bf16[2,128,128]{2,1,0:T(8,128)(2,1)}, bf16[16,128]{1,0:T(8,128)(2,1)}, f32[4,128,128]{2,1,0:T(8,128)}) custom-call(bf16[2,32,256,256]{3,2,1,0:T(8,128)(2,1)} %matrix_hbm.1, bf16[2,32,256,128]{3,2,1,0:T(8,128)(2,1)} %cell_hbm.1, bf16[2,32,256,128]{3,2,1,0:T(8,128)(2,1)} %x_hbm.1, ...), custom_call_target="tpu_custom_call" | custom-call | tf_op jit(solution)/shard_map/mega/pallas_call | solution.py:409
  31.6 3.3 %finish.1 = (bf16[2,32,128,128]{3,2,1,0:T(8,128)(2,1)}, bf16[2,32,128,128]{3,2,1,0:T(8,128)(2,1)}) custom-call(bf16[2,32,128,128]{3,2,1,0:T(8,128)(2,1)} %get-tuple-element.7.x_in, bf16[2,32,128,128]{3,2,1,0:T(8,128)(2,1)} %get-tuple-element.8.y_in, bf16[2,128,128]{2,1,0:T(8,128)(2,1)} %get-tuple-element.9.packed_in, ...), custom_call_target="tpu_custom_call" | custom-call | tf_op jit(solution)/shard_map/finish/pallas_call | solution.py:450

commit v7 on v6

--- a/solution.py
+++ b/solution.py
@@ -38,15 +38,16 @@
 
 def mega(
     matrix_hbm, cell_hbm, x_hbm, y_hbm,
+    x_conduct_hbm, y_conduct_hbm, cell_skel_hbm, x_skel_hbm, y_skel_hbm, cell_rank_hbm, x_rank_hbm, y_rank_hbm,
+    x_out, y_out, late_packed, late_lines, late_part,
     x_conduct, y_conduct, cell_skel, x_skel, y_skel, cell_rank, x_rank, y_rank,
-    x_out, y_out, late_packed, late_lines, late_part,
     matrix, interp, x_interp, y_interp, tops, bottoms, schurs, x_basis, basis, inner, face,
     x_face, y_face, packed, packed_in, diagonals, diagonals_in, lifted, lifted_in, partial,
-    late_sem, in_sem, out_sem, send_sem, recv_sem,
+    small_sem, late_sem, in_sem, out_sem, send_sem, recv_sem,
 ):
     gx, yz = lax.axis_index("gx"), lax.axis_index("yz")
     gxs, yzs = lax.axis_size("gx"), lax.axis_size("yz")
-    nj = cell_skel.shape[1]
+    nj = cell_skel_hbm.shape[1]
     has_down, has_up = gx > 0, gx < gxs - 1
     has_left, has_right = yz > 0, yz < yzs - 1
 
@@ -84,6 +85,17 @@
     def loaded(kind, row, cols):
         copies[kind, row, cols].wait()
 
+    small = []
+
+    def load_small(*pairs):
+        for src, dst in pairs:
+            small.append(pltpu.make_async_copy(src, dst, small_sem.at[len(small)]))
+            small[-1].start()
+
+    load_small(
+        (cell_skel_hbm, cell_skel), (cell_rank_hbm, cell_rank), (x_skel_hbm, x_skel), (x_rank_hbm, x_rank),
+        (x_conduct_hbm, x_conduct),
+    )
     for k, cols in enumerate(upper):
         if k < len(lower):
             load("c", 0, lower[k])
@@ -92,16 +104,6 @@
     load("m", 0, low)
     load("c", 0, high)
     load("m", 0, high)
-    load("c", 1, low)
-    load("m", 1, low)
-    load("m", 1, high)
-    for cols in halves:
-        load("x", 0, cols)
-    for cols in halves:
-        load("y", 0, cols)
-        load("y", 1, cols)
-    load("x", 1, low)
-
     unknowns = lax.broadcasted_iota(jnp.int32, (256, 128), 0).astype(F32).astype(BF16)
     down = lax.broadcasted_iota(jnp.int32, (128, 128), 0)
     across = lax.broadcasted_iota(jnp.int32, (128, 128), 1)
@@ -230,6 +232,8 @@
             pl.when(has_up)(copy.wait_recv)
 
     count = sum(x.astype(jnp.int32) for x in (has_down, has_up, has_left, has_right))
+    for copy in small:
+        copy.wait()
     for k, cols in enumerate(upper):
         if k < len(lower):
             loaded("c", 0, lower[k])
@@ -242,6 +246,17 @@
         cell_bases(1, cols)
         lift_out(cols)
         pl.when(has_up)(lift[k].start)
+    load("c", 1, low)
+    load("m", 1, low)
+    load("m", 1, high)
+    for cols in halves:
+        load("x", 0, cols)
+    for cols in halves:
+        load("y", 0, cols)
+        load("y", 1, cols)
+    load("x", 1, low)
+    early = len(small)
+    load_small((y_skel_hbm, y_skel), (y_rank_hbm, y_rank), (y_conduct_hbm, y_conduct))
     loaded("m", 0, low)
     cell_schurs(0, low)
     for k in range(len(lower)):
@@ -298,6 +313,8 @@
 
     for cols in halves:
         own_faces(0, cols, "x")
+    for copy in small[early:]:
+        copy.wait()
     own_faces(0, halves[0], "y")
     own_faces(1, halves[0], "y")
     answer(0)
@@ -397,8 +414,6 @@
     low, high = LOWER[-1][1] - LOWER[0][0], UPPER[-1][1] - UPPER[0][0]
     most = max(N, low, high)
     hbm = pl.BlockSpec(memory_space=pl.ANY)
-    vmem = pl.BlockSpec(memory_space=pltpu.VMEM)
-    smem = pl.BlockSpec(memory_space=pltpu.SMEM)
     out = jax.ShapeDtypeStruct((2, nj, 128, 128), BF16)
     count = UPPER[-1][1] - UPPER[-1][0]
     late = [
@@ -408,10 +423,18 @@
     ]
     faces = pl.pallas_call(
         mega,
-        in_specs=[hbm] * 4 + [vmem] * 5 + [smem] * 3,
+        in_specs=[hbm] * 12,
         out_specs=[hbm] * 5,
         out_shape=[out] * 2 + late,
         scratch_shapes=[
+            pltpu.VMEM((2, nj, 128), BF16),
+            pltpu.VMEM((2, nj, 128), BF16),
+            pltpu.VMEM((2, nj, 128), jnp.int32),
+            pltpu.VMEM((2, nj, 128), jnp.int32),
+            pltpu.VMEM((2, nj, 128), jnp.int32),
+            pltpu.SMEM((2, nj), jnp.int32),
+            pltpu.SMEM((2, nj), jnp.int32),
+            pltpu.SMEM((2, nj), jnp.int32),
             pltpu.VMEM((2, nj, 256, 256), BF16),
             pltpu.VMEM((2, nj, 256, 128), BF16),
             pltpu.VMEM((2, nj, 256, 128), BF16),
@@ -432,6 +455,7 @@
             pltpu.VMEM((high, 128, 256), BF16),
             pltpu.VMEM((high, 128, 256), BF16),
             pltpu.VMEM((high, 128, 128), F32),
+            pltpu.SemaphoreType.DMA((8,)),
             pltpu.SemaphoreType.DMA((3,)),
             pltpu.SemaphoreType.DMA((21,)),
             pltpu.SemaphoreType.DMA((10,)),

time: 35.3 us -> 34.6 us (0.980)
  Pallas kernels: 34.3 us -> 33.6 us
    pallas_call x1, Pallas kernels: 31 us -> 30.3 us  [body(): pl.pallas_call(mega, in_specs=[hbm] * 12, out_specs=[hbm] * 5, out_shape=...]
where the time goes in v7:
time: 34.6 us; the launch traced here: 34.4 us
  Pallas kernels  33.6 us (97%)
  between operations  0.8 us (2%)
    pallas_call x1, Pallas kernels, body(): pl.pallas_call(mega, in_specs=[hbm] * 12, out_specs=[hbm] * 5, out_shape=...  30.3 us
    pallas_call x1, Pallas kernels, body(): pl.pallas_call(finish, in_specs=[hbm] * 5, out_specs=[hbm] * 2, out_shape...  3.32 us

profile of v7, /device:TPU:90, one launch (start us, length us, event | category | flops | bytes accessed | tf_op | source)
XLA Modules:
  0.0 34.4 jit_solution(17095689034233312199)
XLA Ops:
  0.6 30.3 %mega.1 = (bf16[2,32,128,128]{3,2,1,0:T(8,128)(2,1)}, bf16[2,32,128,128]{3,2,1,0:T(8,128)(2,1)}, bf16[2,128,128]{2,1,0:T(8,128)(2,1)}, bf16[16,128]{1,0:T(8,128)(2,1)}, f32[4,128,128]{2,1,0:T(8,128)}) custom-call(bf16[2,32,256,256]{3,2,1,0:T(8,128)(2,1)} %matrix_hbm.1, bf16[2,32,256,128]{3,2,1,0:T(8,128)(2,1)} %cell_hbm.1, bf16[2,32,256,128]{3,2,1,0:T(8,128)(2,1)} %x_hbm.1, ...), custom_call_target="tpu_custom_call" | custom-call | tf_op jit(solution)/shard_map/mega/pallas_call | solution.py:424
  31.0 3.3 %finish.1 = (bf16[2,32,128,128]{3,2,1,0:T(8,128)(2,1)}, bf16[2,32,128,128]{3,2,1,0:T(8,128)(2,1)}) custom-call(bf16[2,32,128,128]{3,2,1,0:T(8,128)(2,1)} %get-tuple-element.7.x_in, bf16[2,32,128,128]{3,2,1,0:T(8,128)(2,1)} %get-tuple-element.8.y_in, bf16[2,128,128]{2,1,0:T(8,128)(2,1)} %get-tuple-element.9.packed_in, ...), custom_call_target="tpu_custom_call" | custom-call | tf_op jit(solution)/shard_map/finish/pallas_call | solution.py:474

commit v8 on v7

--- a/solution.py
+++ b/solution.py
@@ -92,13 +92,13 @@
             small.append(pltpu.make_async_copy(src, dst, small_sem.at[len(small)]))
             small[-1].start()
 
-    load_small(
-        (cell_skel_hbm, cell_skel), (cell_rank_hbm, cell_rank), (x_skel_hbm, x_skel), (x_rank_hbm, x_rank),
-        (x_conduct_hbm, x_conduct),
-    )
+    load_small((cell_skel_hbm, cell_skel), (cell_rank_hbm, cell_rank))
+    first = len(small)
     for k, cols in enumerate(upper):
         if k < len(lower):
             load("c", 0, lower[k])
+        if k == 0:
+            load_small((x_skel_hbm, x_skel), (x_rank_hbm, x_rank), (x_conduct_hbm, x_conduct))
         load("c", 1, cols)
         load("x", 1, cols)
     load("m", 0, low)
@@ -232,8 +232,9 @@
             pl.when(has_up)(copy.wait_recv)
 
     count = sum(x.astype(jnp.int32) for x in (has_down, has_up, has_left, has_right))
-    for copy in small:
+    for copy in small[:first]:
         copy.wait()
+    middle = len(small)
     for k, cols in enumerate(upper):
         if k < len(lower):
             loaded("c", 0, lower[k])
@@ -241,6 +242,9 @@
             if k == 0:
                 pl.semaphore_wait(barrier, count)
             pl.when(has_down)(top_copy[k].start)
+        if k == 0:
+            for copy in small[first:middle]:
+                copy.wait()
         loaded("c", 1, cols)
         loaded("x", 1, cols)
         cell_bases(1, cols)

time: 34.6 us -> 34.5 us (level)
  no operation moved by 1% of the time
where the time goes in v8:
time: 34.5 us; the launch traced here: 34.4 us
  Pallas kernels  33.6 us (97%)
  between operations  0.8 us (2%)
    pallas_call x1, Pallas kernels, body(): pl.pallas_call(mega, in_specs=[hbm] * 12, out_specs=[hbm] * 5, out_shape=...  30.2 us
    pallas_call x1, Pallas kernels, body(): pl.pallas_call(finish, in_specs=[hbm] * 5, out_specs=[hbm] * 2, out_shape...  3.32 us

profile of v8, /device:TPU:90, one launch (start us, length us, event | category | flops | bytes accessed | tf_op | source)
XLA Modules:
  0.0 34.4 jit_solution(15300332717627116216)
XLA Ops:
  0.6 30.2 %mega.1 = (bf16[2,32,128,128]{3,2,1,0:T(8,128)(2,1)}, bf16[2,32,128,128]{3,2,1,0:T(8,128)(2,1)}, bf16[2,128,128]{2,1,0:T(8,128)(2,1)}, bf16[16,128]{1,0:T(8,128)(2,1)}, f32[4,128,128]{2,1,0:T(8,128)}) custom-call(bf16[2,32,256,256]{3,2,1,0:T(8,128)(2,1)} %matrix_hbm.1, bf16[2,32,256,128]{3,2,1,0:T(8,128)(2,1)} %cell_hbm.1, bf16[2,32,256,128]{3,2,1,0:T(8,128)(2,1)} %x_hbm.1, ...), custom_call_target="tpu_custom_call" | custom-call | tf_op jit(solution)/shard_map/mega/pallas_call | solution.py:428
  30.9 3.3 %finish.1 = (bf16[2,32,128,128]{3,2,1,0:T(8,128)(2,1)}, bf16[2,32,128,128]{3,2,1,0:T(8,128)(2,1)}) custom-call(bf16[2,32,128,128]{3,2,1,0:T(8,128)(2,1)} %get-tuple-element.7.x_in, bf16[2,32,128,128]{3,2,1,0:T(8,128)(2,1)} %get-tuple-element.8.y_in, bf16[2,128,128]{2,1,0:T(8,128)(2,1)} %get-tuple-element.9.packed_in, ...), custom_call_target="tpu_custom_call" | custom-call | tf_op jit(solution)/shard_map/finish/pallas_call | solution.py:478
